TPU v7x, 128 devices: a whole 4x4x4 slice. The times are simulated.
128 devices in a mesh: gx: 32 (over x, z, core), gy: 4 (over y).
Axes of the slice: x: 4, y: 4, z: 4, core: 2. Of those that a mesh axis runs over, the one named last changes fastest.
Arguments:
- forcing: float32 [8, 4096, 1024], P(None, 'gx', 'gy'), may hold values from -120 to 120
- patches: bfloat16 [4096, 512, 128], P('gx', 'gy'), may hold values from -6 to 6
- owners: int32 [4096, 4], P('gx', 'gy'), may hold values from 0 to 127, as said below
- slots: int32 [4096, 4], P('gx', 'gy'), may hold values from 0 to 1
- cond_x: float32 [8, 4096, 1024], P(None, 'gx', 'gy'), may hold values from 0.2 to 5
- cond_y: float32 [8, 4096, 1024], P(None, 'gx', 'gy'), may hold values from 0.2 to 5
- cond_z: float32 [8, 4096, 1024], P(None, 'gx', 'gy'), may hold values from 0.02 to 0.5
- storage: float32 [8, 4096, 1024], P(None, 'gx', 'gy'), may hold values from 0.1 to 1
- fixed: int32 [8, 4096, 1024], P(None, 'gx', 'gy'), may hold values 0 or 1
- closed: int32 [8, 4096, 1024], P(None, 'gx', 'gy'), may hold values 0 or 1
Outputs:
- solution: float32 [8, 4096, 1024], P(None, 'gx', 'gy')
- residual: float32 [8, 4096, 1024], P(None, 'gx', 'gy')
Inputs may be any that keep to these rules, and one draw needn't show every extreme that they name: `owners`: among the 128 patches of one device (entries q of one block of 128 along the first dimension, one column c) no owner appears more than 2 times, and in every device's patches one common owner appears exactly 2 times.
All inputs are finite; a program needn't handle non-finite values. No bound on the sum of `fixed` or of `closed` on one device may be relied on, other than what follows from the above.
Results may differ from a plain program's by a relative error of at most 0.0003.
Values may be sent and summed in bfloat16 or wider, within the bound.
A program may use at most 128 MiB of HBM per device.

v0:
```python
import jax
import jax.numpy as jnp
from jax import lax
from jax.sharding import PartitionSpec as P

CAP = 2
ITERS = 3


def shifted(x, axis, by):
    count = lax.axis_size(axis)
    pairs = [(i, i + by) for i in range(count) if 0 <= i + by < count]
    return lax.ppermute(x, axis, pairs)


def padded_2(block, sides, width):
    for axis, dim in sides:
        count = lax.axis_size(axis)
        forward = [(i, i + 1) for i in range(count - 1)]
        backward = [(target, source) for source, target in forward]
        low = lax.ppermute(
            lax.slice_in_dim(block, block.shape[dim] - width, None, axis=dim), axis, forward
        )
        high = lax.ppermute(lax.slice_in_dim(block, 0, width, axis=dim), axis, backward)
        block = jnp.concatenate([low, block, high], axis=dim)
    return block


def on_device(forcing, patches, owners, slots, cond_x, cond_y, cond_z, storage, fixed, closed):
    layers, tile_rows, tile_cols = forcing.shape
    count_x = lax.axis_size("gx")
    count_y = lax.axis_size("gy")
    devices_all = count_x * count_y
    per_device = patches.shape[0]
    side = patches.shape[1]
    slot_count = tile_cols // side
    owner_list = owners[:, 0]
    slot_list = slots[:, 0]
    targets = jnp.arange(devices_all, dtype=jnp.int32)
    owner_hits = (owner_list[:, None] == targets[None, :]).astype(jnp.float32)
    earlier = (jnp.arange(per_device)[:, None] > jnp.arange(per_device)[None, :]).astype(
        jnp.float32
    )
    before = jnp.dot(earlier, owner_hits, precision=lax.Precision.HIGHEST)
    ranking = jnp.sum(before * owner_hits, axis=1).astype(jnp.int32)
    destination = owner_list * CAP + ranking
    mailbox = jnp.arange(devices_all * CAP, dtype=jnp.int32)
    chosen = mailbox[:, None] == destination[None, :]
    outgoing = jnp.einsum(
        "sp,pab->sab", chosen.astype(jnp.bfloat16), patches, preferred_element_type=jnp.float32
    ).astype(jnp.bfloat16)
    labels = jnp.sum(
        chosen.astype(jnp.float32) * (slot_list + 1).astype(jnp.float32)[None, :], axis=1
    ).astype(jnp.bfloat16)
    arrived, arrived_labels = (
        lax.all_to_all(outgoing, ("gx", "gy"), split_axis=0, concat_axis=0, tiled=True),
        lax.all_to_all(labels, ("gx", "gy"), split_axis=0, concat_axis=0, tiled=True),
    )
    slot_ids = jnp.arange(1, slot_count + 1).astype(jnp.float32)
    placing = (arrived_labels.astype(jnp.float32)[None, :] == slot_ids[:, None]).astype(
        jnp.bfloat16
    )
    placed = jnp.einsum("sm,mab->sab", placing, arrived, preferred_element_type=jnp.float32)
    surface = placed.transpose(1, 0, 2).reshape(side, slot_count * side)
    keep_mask = (1 - fixed).astype(jnp.float32)
    top_layer = forcing[0] + surface
    rhs = keep_mask * jnp.concatenate([top_layer[None], forcing[1:]], axis=0)
    open_faces = (1 - closed).astype(jnp.float32)
    index_x = lax.axis_index("gx")
    index_y = lax.axis_index("gy")
    row_ids = lax.broadcasted_iota(jnp.int32, (1, tile_rows, 1), 1)
    col_ids = lax.broadcasted_iota(jnp.int32, (1, 1, tile_cols), 2)
    layer_ids = lax.broadcasted_iota(jnp.int32, (layers, 1, 1), 0)
    east_edge = (row_ids == tile_rows - 1) & (index_x == count_x - 1)
    north_edge = (col_ids == tile_cols - 1) & (index_y == count_y - 1)
    cond_east = cond_x * open_faces * jnp.where(east_edge, 0.0, 1.0)
    cond_north = cond_y * open_faces * jnp.where(north_edge, 0.0, 1.0)
    cond_above = cond_z * jnp.where(layer_ids == layers - 1, 0.0, 1.0)
    west_rim = shifted(cond_east[:, -1:, :], "gx", 1)
    south_rim = shifted(cond_north[:, :, -1:], "gy", 1)
    cond_west = jnp.concatenate([west_rim, cond_east[:, :-1, :]], axis=1)
    cond_south = jnp.concatenate([south_rim, cond_north[:, :, :-1]], axis=2)
    cond_below = jnp.concatenate([jnp.zeros_like(cond_above[:1]), cond_above[:-1]], axis=0)
    diagonal = storage + cond_east + cond_west + cond_north + cond_south + cond_above + cond_below
    inverse = 1.0 / (keep_mask * diagonal + 1.0 - keep_mask)

    def inner_total(first, second):
        return lax.psum(jnp.sum(first * second), ("gx", "gy"))

    solution = jnp.zeros_like(rhs)
    residual = rhs
    precond = inverse * residual
    direction = precond
    inner = inner_total(residual, precond)
    for iteration in range(ITERS):
        masked = keep_mask * direction
        padded = padded_2(masked, (("gx", 1), ("gy", 2)), 1)
        zero_layer = jnp.zeros_like(masked[:1])
        above_cells = jnp.concatenate([masked[1:], zero_layer], axis=0)
        below_cells = jnp.concatenate([zero_layer, masked[:-1]], axis=0)
        flux = (
            diagonal * masked - cond_east * padded[:, 2:, 1:-1] - cond_west * padded[:, :-2, 1:-1]
        )
        flux = flux - cond_north * padded[:, 1:-1, 2:] - cond_south * padded[:, 1:-1, :-2]
        flux = flux - cond_above * above_cells - cond_below * below_cells
        image = keep_mask * flux + (1.0 - keep_mask) * direction
        step_size = inner / lax.psum(jnp.sum(direction * image), ("gx", "gy"))
        solution = solution + step_size * direction
        residual = residual - step_size * image
        if iteration + 1 < ITERS:
            precond = inverse * residual
            inner_next = inner_total(residual, precond)
            direction = precond + inner_next / inner * direction
            inner = inner_next
    return (solution, residual)


def solution(mesh):
    return jax.shard_map(
        on_device,
        mesh=mesh,
        in_specs=(
            P(None, "gx", "gy"),
            P("gx", "gy", None),
            P("gx", "gy"),
            P("gx", "gy"),
            P(None, "gx", "gy"),
            P(None, "gx", "gy"),
            P(None, "gx", "gy"),
            P(None, "gx", "gy"),
            P(None, "gx", "gy"),
            P(None, "gx", "gy"),
        ),
        out_specs=(P(None, "gx", "gy"), P(None, "gx", "gy")),
        check_vma=False,
    )
```

profile of v0, /device:TPU:1, one launch (start us, length us, event | category | flops | bytes accessed | tf_op | source)
XLA Modules:
  0.0 614.3 jit_solution(8807228088848659126)
XLA Ops:
  0.6 0.9 fusion.6
  3.0 0.8 convert_element_type.73
  3.8 11.5 %all-to-all-start = ((bf16[128,2,1]{1,2,0:T(2,128)(2,1)}), bf16[128,2,1]{1,2,0:T(2,128)(2,1)S(1)}, u32[]{:S(2)}, u32[]{:S(2)}) async-start(bf16[128,2,1]{1,2,0:T(2,128)(2,1)} %convert_element_type.73), calls=%async_computation | async-start | bytes 131072 | tf_op jit(solution)/shard_map/all_to_all | solution.py:57
  15.3 9.5 %convolution_convert_fusion = bf16[256,128,128]{2,0,1:T(8,128)(2,1)} fusion(bf16[128,128,128]{2,1,0:T(8,128)(2,1)} %param.11, s32[128]{0:T(128)S(1)} %convert_add_fusion), kind=kOutput, calls=%fused_computation.2 | convolution fusion | flops 1077968896 | bytes 12583424 | tf_op jit(solution)/shard_map/sp,pab->sab/dot_general | solution.py:49
  24.8 12.0 %copy.57 = bf16[256,128,128]{2,1,0:T(8,128)(2,1)} copy(bf16[256,128,128]{2,0,1:T(8,128)(2,1)} %convolution_convert_fusion) | data formatting | bytes 16777216 | tf_op jit(solution)/shard_map/convert_element_type | solution.py:51
  36.8 10.9 %all-to-all-start.1 = ((bf16[256,128,128]{2,1,0:T(8,128)(2,1)}), bf16[256,128,128]{2,1,0:T(8,128)(2,1)}, u32[]{:S(2)}, u32[]{:S(2)}) async-start(bf16[256,128,128]{2,1,0:T(8,128)(2,1)} %copy.57), calls=%async_computation.1 | async-start | bytes 16777216 | tf_op jit(solution)/shard_map/all_to_all | solution.py:56
  47.7 3.4 fusion.49
  51.1 1.0 slice.162
  52.1 4.1 collective-permute-start.1
  56.2 3.8 collective-permute-start
  60.0 1.0 slice.161
  61.0 1.2 slice-done
  62.2 1.5 copy.80
  63.8 1.6 copy_multiply_fusion
  65.7 86.9 %all-to-all-done.1 = bf16[256,128,128]{2,1,0:T(8,128)(2,1)} async-done(((bf16[256,128,128]{2,1,0:T(8,128)(2,1)}), bf16[256,128,128]{2,1,0:T(8,128)(2,1)}, u32[]{:S(2)}, u32[]{:S(2)}) %all-to-all-start.1) | async-done | bytes 8388640 | tf_op jit(solution)/shard_map/all_to_all | solution.py:56
  152.5 7.9 %fusion.3 = f32[128,2,128]{2,1,0:T(2,128)S(1)} fusion(bf16[256,128,128]{2,1,0:T(8,128)(2,1)} %all-to-all-done.1, f32[256]{0:T(256)S(1)} %reshape.77, f32[2]{0:T(128)S(1)} %add_convert_fusion), kind=kOutput, calls=%fused_computation.4 | convolution fusion | flops 16777728 | bytes 8520712 | tf_op jit(solution)/shard_map/sm,mab->sab/dot_general | solution.py:63
  160.6 0.9 slice_add_fusion
  161.7 6.8 %fusion.54 = (f32[8,128,256]{2,0,1:T(8,128)S(1)}, f32[8,128,256]{2,0,1:T(8,128)}, f32[8,128,256]{2,0,1:T(8,128)}, f32[8,128,256]{2,0,1:T(8,128)}) fusion(s32[8,128,256]{2,1,0:T(8,128)S(1)} %copy-done, f32[7,128,256]{2,0,1:T(8,128)} %copy.80, f32[1,128,256]{2,0,1:T(1,128)S(1)} %copy.60, f32[7,128,256]{2,0,1:T(8,128)} %bitcast.18, ...), kind=kLoop, calls=%fused_computation.103 | loop fusion | flops 4980736 | bytes 13500448 | tf_op jit(solution)/shard_map/mul | solution.py:96
  168.5 1.9 collective-permute-start.2
  170.4 3.8 collective-permute-start.3
  175.0 1.1 fusion.68
  176.1 1.4 copy.68
  177.5 1.3 collective-permute-start.5
  178.8 1.4 copy.66
  180.2 1.3 collective-permute-start.4
  181.5 3.0 fusion.74
  184.5 1.2 copy.69
  185.7 1.2 copy.67
  186.9 11.3 %multiply_reduce_fusion.4 = (f32[]{:T(128)}, f32[]{:T(128)}, f32[8,128,256]{2,0,1:T(8,128)}) fusion(f32[8,128,256]{2,0,1:T(8,128)} %get-tuple-element.28, f32[8,128,256]{2,0,1:T(8,128)} %get-tuple-element.29, f32[7,128,256]{2,0,1:T(8,128)} %get-tuple-element.48, f32[7,128,256]{2,0,1:T(8,128)} %get-tuple-element.47, ...), kind=kLoop, calls=%fused_computation.98 | loop fusion | flops 10485758 | bytes 14311592 | tf_op jit(solution)/shard_map/reduce_sum | solution.py:107
  198.3 68.1 %all-reduce.7 = (f32[]{:T(128)}, f32[]{:T(128)}) all-reduce(f32[]{:T(128)} %get-tuple-element.9, f32[]{:T(128)} %get-tuple-element.8), channel_id=1, replica_groups=mesh['gx'=32,'gy'=4] {'gx','gy'}, use_global_device_ids=true, to_apply=%region_3.4 | all-reduce | flops 2 | bytes 16 | tf_op jit(solution)/shard_map/psum | solution.py:88
  267.7 4.0 multiply_reduce_fusion.3
  271.7 62.5 %psum.44 = f32[]{:T(128)} all-reduce(f32[]{:T(128)} %get-tuple-element.23), channel_id=1, replica_groups=mesh['gx'=32,'gy'=4] {'gx','gy'}, use_global_device_ids=true, to_apply=%region_7.8 | all-reduce | flops 1 | bytes 8 | tf_op jit(solution)/shard_map/psum | solution.py:88
  335.5 3.2 fusion.52
  338.8 2.5 collective-permute-start.6
  341.3 3.1 collective-permute-start.7
  344.3 0.8 collective-permute-done.7
  345.2 1.1 fusion.67
  346.3 1.4 copy.72
  347.7 3.2 collective-permute-start.9
  350.9 1.4 copy.70
  352.2 1.3 collective-permute-start.8
  353.5 3.1 fusion.72
  356.7 1.1 copy.73
  357.8 1.2 copy.71
  359.0 10.0 %multiply_reduce_fusion.2 = (f32[]{:T(128)}, f32[8,128,256]{2,0,1:T(8,128)}) fusion(f32[8,128,256]{2,0,1:T(8,128)} %get-tuple-element.22, f32[7,128,256]{2,0,1:T(8,128)} %get-tuple-element.44, f32[7,128,256]{2,0,1:T(8,128)} %get-tuple-element.43, f32[8,1,256]{2,0,1:T(8,128)S(1)} %collective-permute-done.6, f32[8,128,256]{2,0,1:T(8,128)} %copy-done.3, ...), kind=kLoop, calls=%fused_computation.94 | loop fusion | flops 9961471 | bytes 13263012 | tf_op jit(solution)/shard_map/reduce_sum | solution.py:107
  369.1 67.3 %psum.45 = f32[]{:T(128)} all-reduce(f32[]{:T(128)} %get-tuple-element.19), channel_id=1, replica_groups=mesh['gx'=32,'gy'=4] {'gx','gy'}, use_global_device_ids=true, to_apply=%region_9.10 | all-reduce | flops 1 | bytes 8 | tf_op jit(solution)/shard_map/psum | solution.py:107
  437.7 4.2 multiply_reduce_fusion.1
  441.8 63.2 %psum.46 = f32[]{:T(128)} all-reduce(f32[]{:T(128)} %get-tuple-element.16), channel_id=1, replica_groups=mesh['gx'=32,'gy'=4] {'gx','gy'}, use_global_device_ids=true, to_apply=%region_11.12 | all-reduce | flops 1 | bytes 8 | tf_op jit(solution)/shard_map/psum | solution.py:88
  506.4 3.3 fusion.53
  509.6 2.8 collective-permute-start.10
  512.5 2.7 collective-permute-start.11
  516.0 1.1 fusion.66
  517.2 1.4 copy.76
  518.6 1.9 collective-permute-start.13
  520.4 1.4 copy.74
  521.8 1.3 collective-permute-start.12
  523.1 3.1 fusion.70
  526.2 1.1 copy.77
  527.3 1.2 copy.75
  528.6 10.1 %multiply_reduce_fusion = (f32[]{:T(128)}, f32[8,128,256]{2,0,1:T(8,128)}) fusion(f32[8,128,256]{2,0,1:T(8,128)} %get-tuple-element.15, f32[7,128,256]{2,0,1:T(8,128)} %get-tuple-element.40, f32[7,128,256]{2,0,1:T(8,128)} %get-tuple-element.39, f32[8,1,256]{2,0,1:T(8,128)S(1)} %collective-permute-done.10, f32[8,128,256]{2,0,1:T(8,128)} %copy-done.2, ...), kind=kLoop, calls=%fused_computation.90 | loop fusion | flops 9961471 | bytes 13263012 | tf_op jit(solution)/shard_map/reduce_sum | solution.py:107
  538.7 68.5 %psum.47 = f32[]{:T(128)} all-reduce(f32[]{:T(128)} %get-tuple-element.12), channel_id=1, replica_groups=mesh['gx'=32,'gy'=4] {'gx','gy'}, use_global_device_ids=true, to_apply=%region_13.14 | all-reduce | flops 1 | bytes 8 | tf_op jit(solution)/shard_map/psum | solution.py:107
  608.6 2.8 multiply_subtract_fusion
  611.5 1.3 copy.78
  612.7 1.3 copy.79
  (45 shorter events, 3.6 us)
Async XLA Ops:
  3.8 33.0 %all-to-all-start = ((bf16[128,2,1]{1,2,0:T(2,128)(2,1)}), bf16[128,2,1]{1,2,0:T(2,128)(2,1)S(1)}, u32[]{:S(2)}, u32[]{:S(2)}) async-start(bf16[128,2,1]{1,2,0:T(2,128)(2,1)} %convert_element_type.73), calls=%async_computation | async-start | bytes 131072 | tf_op jit(solution)/shard_map/all_to_all | solution.py:57
  36.8 10.9 %copy-start.5 = (f32[8,128,256]{2,1,0:T(8,128)S(1)}, f32[8,128,256]{2,1,0:T(8,128)}, u32[]{:S(2)}) copy-start(f32[8,128,256]{2,1,0:T(8,128)} %param.14) | copy-start | bytes 3145732
  36.8 115.7 %all-to-all-start.1 = ((bf16[256,128,128]{2,1,0:T(8,128)(2,1)}), bf16[256,128,128]{2,1,0:T(8,128)(2,1)}, u32[]{:S(2)}, u32[]{:S(2)}) async-start(bf16[256,128,128]{2,1,0:T(8,128)(2,1)} %copy.57), calls=%async_computation.1 | async-start | bytes 16777216 | tf_op jit(solution)/shard_map/all_to_all | solution.py:56
  52.1 109.6 %collective-permute-start.1 = (f32[8,128,1]{2,0,1:T(8,128)}, f32[8,128,1]{2,0,1:T(8,128)}, u32[]{:S(2)}, u32[]{:S(2)}) collective-permute-start(f32[8,128,1]{2,0,1:T(8,128)} %slice.162), channel_id=1, source_target_pairs={{0,1},{1,2},{2,3},{4,5},{5,6},{6,7},{8,9},{9,10},{10,11},{12,13},{... | collective-permute-start | bytes 12296 | tf_op jit(solution)/shard_map/ppermute | solution.py:13
  56.2 105.5 %collective-permute-start = (f32[8,1,256]{2,0,1:T(8,128)S(1)}, f32[8,1,256]{2,0,1:T(8,128)S(1)}, u32[]{:S(2)}, u32[]{:S(2)}) collective-permute-start(f32[8,1,256]{2,0,1:T(8,128)S(1)} %slice.160), channel_id=1, source_target_pairs={{0,4},{4,8},{8,12},{12,16},{16,20},{20,24},{24,28},{28,32},{32,36}... | collective-permute-start | bytes 24584 | tf_op jit(solution)/shard_map/ppermute | solution.py:13
  61.0 1.2 slice-start
  62.2 1.5 copy-start.4
  152.5 9.2 %copy-start = (s32[8,128,256]{2,1,0:T(8,128)S(1)}, s32[8,128,256]{2,1,0:T(8,128)}, u32[]{:S(2)}) copy-start(s32[8,128,256]{2,1,0:T(8,128)} %param.18) | copy-start | bytes 3145732
  168.5 6.4 %copy-start.1 = (f32[8,128,256]{2,0,1:T(8,128)}, f32[8,128,256]{2,0,1:T(8,128)S(1)}, u32[]{:S(2)}) copy-start(f32[8,128,256]{2,0,1:T(8,128)S(1)} %get-tuple-element.27) | copy-start | bytes 3145732
  168.5 5.7 collective-permute-start.2
  170.4 4.4 collective-permute-start.3
  177.5 7.1 %collective-permute-start.5 = (f32[8,130,1]{1,0,2:T(8,128)S(1)}, f32[8,130,1]{1,0,2:T(8,128)S(1)}, u32[]{:S(2)}, u32[]{:S(2)}) collective-permute-start(f32[8,130,1]{1,0,2:T(8,128)S(1)} %copy.68), channel_id=1, source_target_pairs={{0,1},{1,2},{2,3},{4,5},{5,6},{6,7},{8,9},{9,10},{10,11},{12,13},{... | collective-permute-start | bytes 12488 | tf_op jit(solution)/shard_map/ppermute | solution.py:21
  180.2 5.5 collective-permute-start.4
  338.8 6.4 %copy-start.3 = (f32[8,128,256]{2,0,1:T(8,128)}, f32[8,128,256]{2,0,1:T(8,128)S(1)}, u32[]{:S(2)}) copy-start(f32[8,128,256]{2,0,1:T(8,128)S(1)} %get-tuple-element.21) | copy-start | bytes 3145732
  338.8 5.6 collective-permute-start.6
  341.3 3.8 collective-permute-start.7
  347.7 9.0 %collective-permute-start.9 = (f32[8,130,1]{1,0,2:T(8,128)S(1)}, f32[8,130,1]{1,0,2:T(8,128)S(1)}, u32[]{:S(2)}, u32[]{:S(2)}) collective-permute-start(f32[8,130,1]{1,0,2:T(8,128)S(1)} %copy.72), channel_id=1, source_target_pairs={{0,1},{1,2},{2,3},{4,5},{5,6},{6,7},{8,9},{9,10},{10,11},{12,13},{... | collective-permute-start | bytes 12488 | tf_op jit(solution)/shard_map/ppermute | solution.py:21
  352.2 5.6 collective-permute-start.8
  509.6 6.4 %copy-start.2 = (f32[8,128,256]{2,0,1:T(8,128)}, f32[8,128,256]{2,0,1:T(8,128)S(1)}, u32[]{:S(2)}) copy-start(f32[8,128,256]{2,0,1:T(8,128)S(1)} %get-tuple-element.14) | copy-start | bytes 3145732
  509.6 5.6 collective-permute-start.10
  512.5 3.5 collective-permute-start.11
  518.6 7.6 %collective-permute-start.13 = (f32[8,130,1]{1,0,2:T(8,128)S(1)}, f32[8,130,1]{1,0,2:T(8,128)S(1)}, u32[]{:S(2)}, u32[]{:S(2)}) collective-permute-start(f32[8,130,1]{1,0,2:T(8,128)S(1)} %copy.76), channel_id=1, source_target_pairs={{0,1},{1,2},{2,3},{4,5},{5,6},{6,7},{8,9},{9,10},{10,11},{12,13},{... | collective-permute-start | bytes 12488 | tf_op jit(solution)/shard_map/ppermute | solution.py:21
  521.8 5.5 collective-permute-start.12
where the time goes:
time: 624 us; the launch traced here: 614 us
  blocking collectives  330 us (53%)
  waiting for transfers between devices  89 us (14%)
  other arithmetic  63.5 us (10%)
  starting transfers between devices  57.4 us (9%)
  local copies, waits for them, and re-layouts  48.5 us (8%)
  matrix products  18.4 us (3%)
  between operations  7.78 us (1%)
    psum x3, blocking collectives, inner_total(): return lax.psum(jnp.sum(first * second), ('gx', 'gy'))  194 us
    psum x2, blocking collectives, on_device(): step_size = inner / lax.psum(jnp.sum(direction * image), ('gx', 'gy'))  136 us
    all_to_all x1, waiting for transfers between devices, on_device(): lax.all_to_all(outgoing, ('gx', 'gy'), split_axis=0, concat_axis=0, tiled...  86.9 us
    reduce_sum x3, other arithmetic, on_device(): step_size = inner / lax.psum(jnp.sum(direction * image), ('gx', 'gy'))  31.5 us
    ppermute x6, starting transfers between devices, padded_2(): lax.ppermute(lax.slice_in_dim(block, block.shape[dim] - width, None, axis...  16 us
    mul x3, other arithmetic, on_device(): masked = keep_mask * direction  13.3 us
  transfers between devices with their start and end apart: 16, of which 4 were waited for; matrix products, arithmetic and copies ran while one was open for 9% of the time, Pallas kernels for 0%

commit v1 on v0

v1 whole, which is shorter than its diff:
```python
import functools

import jax
import jax.numpy as jnp
from jax import lax
from jax.experimental import pallas as pl
from jax.experimental.pallas import tpu as pltpu
from jax.sharding import PartitionSpec as P

CAP = 2
MESH = pl.DeviceIdType.MESH
PAD = 8
MIB = 1 << 20


class Layout:
    def __init__(self, count_x, count_y):
        self.cores = 2 if count_x % 2 == 0 else 1
        chips = count_x // self.cores
        self.nz = 4 if chips % 4 == 0 else chips
        self.nx = chips // self.nz
        self.ny = count_y

    def me(self):
        gx, gy = lax.axis_index("gx"), lax.axis_index("gy")
        core = gx % self.cores
        chip = gx // self.cores
        return chip // self.nz, chip % self.nz, core, gy

    def device(self, x, z, core, y):
        return ((x * self.nz + z) * self.cores + core, y)

    def moved(self, dx=0, dz=0, dc=0, dy=0):
        x, z, core, y = self.me()
        return self.device(
            (x + dx) % self.nx, (z + dz) % self.nz, (core + dc) % self.cores, (y + dy) % self.ny
        )

    def stages(self):
        first = [
            dict(dc=c, dy=y) for c in range(self.cores) for y in range(self.ny) if (c, y) != (0, 0)
        ]
        return [s for s in (first, [dict(dz=d) for d in range(1, self.nz)],
                            [dict(dx=d) for d in range(1, self.nx)]) if s]


def remote(src, dst, send, recv, device):
    return pltpu.make_async_remote_copy(
        src_ref=src, dst_ref=dst, send_sem=send, recv_sem=recv, device_id=device, device_id_type=MESH
    )


def cg_body(
    lay, count_x, count_y, surface, forcing, cond_x, cond_y, cond_z, storage, fixed, closed,
    solution, residual, tees, east, north, south, above, inverse, enns, col_out, col_in,
    partial, gathered, halo_send, halo_recv, sum_send, sum_recv,
):
    layers, rows, cols = forcing.shape
    step = 32
    blocks = rows // step
    gx, gy = lax.axis_index("gx"), lax.axis_index("gy")
    right = ((gx + 1) % count_x, gy)
    left = ((gx + count_x - 1) % count_x, gy)
    up = (gx, (gy + 1) % count_y)
    down = (gx, (gy + count_y - 1) % count_y)
    lanes = lax.broadcasted_iota(jnp.int32, (step, cols), 1)
    first_lane, last_lane = lanes == 0, lanes == cols - 1
    row_ids = lax.broadcasted_iota(jnp.int32, (rows, rows), 0)
    eye = row_ids == lax.broadcasted_iota(jnp.int32, (rows, rows), 1)

    def east_scale(block):
        last = jnp.where(gx == count_x - 1, 0.0, 1.0).astype(jnp.float32)
        ids = lax.broadcasted_iota(jnp.int32, (step, cols), 0) + block * step
        return jnp.where(ids == rows - 1, last, 1.0)

    north_last = jnp.where(gy == count_y - 1, 0.0, 1.0).astype(jnp.float32)
    north_scale = jnp.where(last_lane, north_last, 1.0)

    def column(block):
        wide = jnp.broadcast_to(block, (rows, rows))
        return jnp.sum(jnp.where(eye, wide, 0.0), axis=0, keepdims=True)

    def uncolumn(row, block):
        wide = jnp.broadcast_to(row, (step, rows))
        mask = eye[block * step : (block + 1) * step]
        return jnp.sum(jnp.where(mask, wide, 0.0), axis=1, keepdims=True)

    def faces(layer, carry):
        for b in range(blocks):
            at = pl.ds(b * step, step)
            open_faces = (1 - closed[layer, at, :]).astype(jnp.float32)
            east[layer, pl.ds(PAD + b * step, step), :] = (
                cond_x[layer, at, :] * open_faces * east_scale(b)
            )
            north[layer, at, :] = cond_y[layer, at, :] * open_faces * north_scale
        above[layer + 1] = cond_z[layer] * jnp.where(layer == layers - 1, 0.0, 1.0)
        col_out[0, 0, pl.ds(layer, 1), :] = column(north[layer, :, cols - 1 : cols])
        return carry

    above[0] = jnp.zeros((rows, cols), jnp.float32)
    lax.fori_loop(0, layers, faces, 0)
    rim_x = remote(
        east.at[:, pl.ds(PAD + rows - 1, 1), :], east.at[:, pl.ds(PAD - 1, 1), :],
        halo_send.at[0, 0], halo_recv.at[0, 0], right,
    )
    rim_y = remote(
        col_out.at[0, 0], col_in.at[0, 0], halo_send.at[0, 1], halo_recv.at[0, 1], up
    )
    rim_x.start()
    rim_y.start()
    rim_x.wait()
    rim_y.wait()

    def prepare(layer, total):
        south_row = col_in[0, 0, pl.ds(layer, 1), :]
        for b in range(blocks):
            at = pl.ds(b * step, step)
            north_here = north[layer, at, :]
            south_here = jnp.where(
                first_lane, uncolumn(south_row, b), pltpu.roll(north_here, 1, 1)
            )
            south[layer, at, :] = south_here
            keep = (1 - fixed[layer, at, :]).astype(jnp.float32)
            diagonal = (
                storage[layer, at, :]
                + east[layer, pl.ds(PAD + b * step, step), :]
                + east[layer, pl.ds(PAD - 1 + b * step, step), :]
                + north_here + south_here + above[layer + 1, at, :] + above[layer, at, :]
            )
            inv = keep / diagonal
            inverse[layer, at, :] = inv
            extra = surface[at, :] * jnp.where(layer == 0, 1.0, 0.0)
            start = keep * (forcing[layer, at, :] + extra)
            enns[0, layer, at, :] = start
            tee = inv * start
            tees[0, layer, pl.ds(PAD + b * step, step), :] = tee
            total = total + fold(tee * start)
        return total

    def fold(x):
        parts = [x[i * 8 : (i + 1) * 8] for i in range(step // 8)]
        while len(parts) > 1:
            parts = [a + b for a, b in zip(parts[::2], parts[1::2])]
        return parts[0]

    zero = jnp.zeros((8, cols), jnp.float32)
    moments = [lax.fori_loop(0, layers, prepare, zero)]

    for j in range(3):
        def borders(layer, carry, j=j):
            here = tees.at[j, layer, pl.ds(PAD, rows), :]
            col_out[j + 1, 0, pl.ds(layer, 1), :] = column(here[:, cols - 1 : cols])
            col_out[j + 1, 1, pl.ds(layer, 1), :] = column(here[:, 0:1])
            return carry

        lax.fori_loop(0, layers, borders, 0)
        copies = [
            remote(tees.at[j, :, pl.ds(PAD + rows - 1, 1), :], tees.at[j, :, pl.ds(PAD - 1, 1), :],
                   halo_send.at[j + 1, 0], halo_recv.at[j + 1, 0], right),
            remote(tees.at[j, :, pl.ds(PAD, 1), :], tees.at[j, :, pl.ds(PAD + rows, 1), :],
                   halo_send.at[j + 1, 1], halo_recv.at[j + 1, 1], left),
            remote(col_out.at[j + 1, 0], col_in.at[j + 1, 0],
                   halo_send.at[j + 1, 2], halo_recv.at[j + 1, 2], up),
            remote(col_out.at[j + 1, 1], col_in.at[j + 1, 1],
                   halo_send.at[j + 1, 3], halo_recv.at[j + 1, 3], down),
        ]
        for copy in copies:
            copy.start()
        for copy in copies:
            copy.wait()

        def apply(layer, carry, j=j):
            odd, even = carry
            south_row = col_in[j + 1, 0, pl.ds(layer, 1), :]
            north_row = col_in[j + 1, 1, pl.ds(layer, 1), :]
            higher = jnp.minimum(layer + 1, layers - 1)
            lower = jnp.maximum(layer - 1, 0)
            for b in range(blocks):
                at = pl.ds(b * step, step)
                mid = pl.ds(PAD + b * step, step)
                here = tees[j, layer, mid, :]
                north_val = jnp.where(
                    last_lane, uncolumn(north_row, b), pltpu.roll(here, cols - 1, 1)
                )
                south_val = jnp.where(first_lane, uncolumn(south_row, b), pltpu.roll(here, 1, 1))
                flux = east[layer, mid, :] * tees[j, layer, pl.ds(PAD + 1 + b * step, step), :]
                flux += (east[layer, pl.ds(PAD - 1 + b * step, step), :]
                         * tees[j, layer, pl.ds(PAD - 1 + b * step, step), :])
                flux += north[layer, at, :] * north_val + south[layer, at, :] * south_val
                flux += above[layer + 1, at, :] * tees[j, higher, mid, :]
                flux += above[layer, at, :] * tees[j, lower, mid, :]
                enns[j + 1, layer, at, :] = flux
                odd = odd + fold(here * flux)
                if j < 2:
                    tee = inverse[layer, at, :] * flux
                    tees[j + 1, layer, mid, :] = tee
                    even = even + fold(tee * flux)
            return odd, even

        odd, even = lax.fori_loop(0, layers, apply, (zero, zero))
        moments.append(odd)
        if j < 2:
            moments.append(even)

    partial[0] = jnp.zeros((8, 128), jnp.float32)
    for k, value in enumerate(moments):
        both = sum(value[:, i * 128 : (i + 1) * 128] for i in range(cols // 128))
        partial[0, k : k + 1, :] = jnp.sum(both, axis=0, keepdims=True)
    base = 0
    for s, peers in enumerate(lay.stages()):
        copies = [
            remote(partial.at[s], gathered.at[base + i], sum_send.at[base + i],
                   sum_recv.at[base + i], lay.moved(**offset))
            for i, offset in enumerate(peers)
        ]
        for copy in copies:
            copy.start()
        for copy in copies:
            copy.wait()
        total = partial[s]
        for i in range(len(peers)):
            total = total + gathered[base + i]
        base += len(peers)
        partial[s + 1] = total
    total = partial[len(lay.stages())]
    sol_w, res_w = scalars(total)

    def finish(layer, carry):
        for b in range(blocks):
            at = pl.ds(b * step, step)
            mid = pl.ds(PAD + b * step, step)
            keep = (1 - fixed[layer, at, :]).astype(jnp.float32)
            out = sol_w[0] * tees[0, layer, mid, :]
            for j in range(1, 3):
                out += sol_w[j] * tees[j, layer, mid, :]
            solution[layer, at, :] = out
            out = res_w[0] * enns[0, layer, at, :]
            for j in range(1, 4):
                out += res_w[j] * enns[j, layer, at, :]
            residual[layer, at, :] = keep * out
        return carry

    lax.fori_loop(0, layers, finish, 0)


def scalars(total):
    def reduce(row):
        return jnp.sum(row, axis=1, keepdims=True)

    rows = [total[k : k + 1, :] for k in range(6)]
    m0, m1 = reduce(rows[0]), reduce(rows[1])
    shift = jnp.where(m1 > 0.5 * m0, 1.0, 0.0)
    scale = 1.0 - shift
    c, current = [m0], rows
    for _ in range(5):
        current = [current[q + 1] - shift * current[q] for q in range(len(current) - 1)]
        c.append(reduce(current[0]))
    d = [scale * c[k] - c[k + 1] for k in range(5)]
    zero = jnp.zeros_like(m0)
    rho, pi, sol = [zero + 1.0], [zero + 1.0], [zero, zero, zero]
    inner = m0
    for i in range(3):
        curve = zero
        for a in range(len(pi)):
            for b in range(len(pi)):
                curve = curve + pi[a] * pi[b] * d[a + b]
        alpha = inner / curve
        for a in range(len(pi)):
            sol[a] = sol[a] + alpha * pi[a]
        rho = rho + [zero]
        for a in range(len(pi)):
            rho[a] = rho[a] - alpha * scale * pi[a]
            rho[a + 1] = rho[a + 1] + alpha * pi[a]
        if i < 2:
            inner_next = zero
            for a in range(len(rho)):
                for b in range(len(rho)):
                    inner_next = inner_next + rho[a] * rho[b] * c[a + b]
            beta = inner_next / inner
            pi = [rho[a] + beta * pi[a] if a < len(pi) else rho[a] for a in range(len(rho))]
            inner = inner_next

    def unshift(w):
        out = [zero] * len(w)
        for k in reversed(range(len(w))):
            moved = [zero] + out[:-1]
            out = [moved[i] - shift * out[i] for i in range(len(w))]
            out[0] = out[0] + w[k]
        return out

    return unshift(sol), unshift(rho)


def cg_kernel(lay, count_x, count_y, *refs):
    barrier = pltpu.get_barrier_semaphore()
    gx, gy = lax.axis_index("gx"), lax.axis_index("gy")
    friends = [((gx + 1) % count_x, gy), ((gx + count_x - 1) % count_x, gy),
               (gx, (gy + 1) % count_y), (gx, (gy + count_y - 1) % count_y)]
    for peers in lay.stages():
        friends += [lay.moved(**offset) for offset in peers]
    for friend in friends:
        pl.semaphore_signal(barrier, inc=1, device_id=friend, device_id_type=MESH)
    pl.semaphore_wait(barrier, len(friends))
    cg_body(lay, count_x, count_y, *refs)


def cg(lay, count_x, count_y, *args):
    layers, rows, cols = args[1].shape
    stages = lay.stages()
    peers = sum(len(s) for s in stages)
    full = lambda *lead: pltpu.VMEM((*lead, layers, rows, cols), jnp.float32)
    padded = lambda *lead: pltpu.VMEM((*lead, layers, rows + 2 * PAD, cols), jnp.float32)
    return pl.pallas_call(
        functools.partial(cg_kernel, lay, count_x, count_y),
        out_shape=[jax.ShapeDtypeStruct((layers, rows, cols), jnp.float32)] * 2,
        in_specs=[pl.BlockSpec(memory_space=pltpu.VMEM)] * len(args),
        out_specs=[pl.BlockSpec(memory_space=pltpu.VMEM)] * 2,
        scratch_shapes=[
            padded(3), padded(), full(), full(),
            pltpu.VMEM((layers + 1, rows, cols), jnp.float32), full(), full(4),
            pltpu.VMEM((4, 2, layers, rows), jnp.float32),
            pltpu.VMEM((4, 2, layers, rows), jnp.float32),
            pltpu.VMEM((len(stages) + 1, 8, 128), jnp.float32),
            pltpu.VMEM((peers, 8, 128), jnp.float32),
            pltpu.SemaphoreType.DMA((4, 4)), pltpu.SemaphoreType.DMA((4, 4)),
            pltpu.SemaphoreType.DMA((peers,)), pltpu.SemaphoreType.DMA((peers,)),
        ],
        compiler_params=pltpu.CompilerParams(
            collective_id=1, has_side_effects=True, vmem_limit_bytes=48 * MIB
        ),
    )(*args)


def exchange(patches, owners, slots, tile_cols):
    count_x = lax.axis_size("gx")
    count_y = lax.axis_size("gy")
    devices_all = count_x * count_y
    per_device = patches.shape[0]
    side = patches.shape[1]
    slot_count = tile_cols // side
    owner_list = owners[:, 0]
    slot_list = slots[:, 0]
    targets = jnp.arange(devices_all, dtype=jnp.int32)
    owner_hits = (owner_list[:, None] == targets[None, :]).astype(jnp.float32)
    earlier = (jnp.arange(per_device)[:, None] > jnp.arange(per_device)[None, :]).astype(
        jnp.float32
    )
    before = jnp.dot(earlier, owner_hits, precision=lax.Precision.HIGHEST)
    ranking = jnp.sum(before * owner_hits, axis=1).astype(jnp.int32)
    destination = owner_list * CAP + ranking
    mailbox = jnp.arange(devices_all * CAP, dtype=jnp.int32)
    chosen = mailbox[:, None] == destination[None, :]
    outgoing = jnp.einsum(
        "sp,pab->sab", chosen.astype(jnp.bfloat16), patches, preferred_element_type=jnp.float32
    ).astype(jnp.bfloat16)
    labels = jnp.sum(
        chosen.astype(jnp.float32) * (slot_list + 1).astype(jnp.float32)[None, :], axis=1
    ).astype(jnp.bfloat16)
    arrived, arrived_labels = (
        lax.all_to_all(outgoing, ("gx", "gy"), split_axis=0, concat_axis=0, tiled=True),
        lax.all_to_all(labels, ("gx", "gy"), split_axis=0, concat_axis=0, tiled=True),
    )
    slot_ids = jnp.arange(1, slot_count + 1).astype(jnp.float32)
    placing = (arrived_labels.astype(jnp.float32)[None, :] == slot_ids[:, None]).astype(
        jnp.bfloat16
    )
    placed = jnp.einsum("sm,mab->sab", placing, arrived, preferred_element_type=jnp.float32)
    return placed.transpose(1, 0, 2).reshape(side, slot_count * side)


def on_device(forcing, patches, owners, slots, cond_x, cond_y, cond_z, storage, fixed, closed):
    count_x, count_y = lax.axis_size("gx"), lax.axis_size("gy")
    lay = Layout(count_x, count_y)
    surface = exchange(patches, owners, slots, forcing.shape[2])
    return tuple(
        cg(lay, count_x, count_y, surface, forcing, cond_x, cond_y, cond_z, storage, fixed, closed)
    )


def solution(mesh):
    grid = P(None, "gx", "gy")
    return jax.shard_map(
        on_device,
        mesh=mesh,
        in_specs=(grid, P("gx", "gy", None), P("gx", "gy"), P("gx", "gy")) + (grid,) * 6,
        out_specs=(grid, grid),
        check_vma=False,
    )
```

time: 624 us -> 205 us (0.33); the launches traced: 614 us -> 204 us
  blocking collectives: 330 us -> 0 us
  other arithmetic: 63.5 us -> 1.63 us
  Pallas kernels: 0 us -> 42.7 us
  starting transfers between devices: 57.4 us -> 21.7 us
  local copies, waits for them, and re-layouts: 48.5 us -> 14.9 us
  waiting for transfers between devices: 89 us -> 104 us
  between operations: 7.78 us -> 0.73 us
    psum x5 -> x0, blocking collectives: 330 us -> none  [the longest x3 194 us: inner_total(): return lax.psum(jnp.sum(first * second), ('gx', 'gy'))]
    pallas_call x0 -> x1, Pallas kernels: none -> 42.7 us  [cg(): pl.pallas_call(functools.partial(cg_kernel, lay, count_x, count_y), out_s...]
    reduce_sum x6 -> x1, other arithmetic: 39.8 us -> 0.12 us  [exchange(): jnp.sum(chosen.astype(jnp.float32) * (slot_list + 1).astype(jnp.float32)[...]
    ppermute x14 -> x0, starting transfers between devices: 35 us -> none  [the longest x6 16 us: padded_2(): lax.ppermute(lax.slice_in_dim(block, block.shape[dim] - width, None, axis...]
    slice x20 -> x0, local copies, waits for them, and re-layouts: 24.1 us -> none  [the longest x3 9.22 us: on_device(): above_cells = jnp.concatenate([masked[1:], zero_layer], axis=0)]
    mul x5 -> x0, other arithmetic: 18.3 us -> none  [the longest x3 13.3 us: on_device(): masked = keep_mask * direction]
    all_to_all x2, waiting for transfers between devices: 86.9 us -> 104 us  [the longest x1 104 us: exchange(): lax.all_to_all(outgoing, ('gx', 'gy'), split_axis=0, concat_axis=0, tiled...]
    ppermute x6 -> x0, local copies, waits for them, and re-layouts: 7.11 us -> none  [the longest x3 3.62 us: padded_2(): lax.ppermute(lax.slice_in_dim(block, 0, width, axis=dim), axis, backward)]
  transfers between devices with their start and end apart: 16 -> 2, of which waited for: 4 -> 1; matrix products, arithmetic and copies ran while one was open for 9% -> 11% of each run, Pallas kernels for 0% -> 0%
where the time goes in v1:
time: 205 us; the launch traced here: 204 us
  waiting for transfers between devices  104 us (51%)
  Pallas kernels  42.7 us (21%)
  starting transfers between devices  21.7 us (11%)
  matrix products  18.3 us (9%)
  local copies, waits for them, and re-layouts  14.9 us (7%)
    all_to_all x1, waiting for transfers between devices, exchange(): lax.all_to_all(outgoing, ('gx', 'gy'), split_axis=0, concat_axis=0, tiled...  104 us
    pallas_call x1, Pallas kernels, cg(): pl.pallas_call(functools.partial(cg_kernel, lay, count_x, count_y), out_s...  42.7 us
    convert_element_type x1, local copies, waits for them, and re-layouts, exchange(): outgoing = jnp.einsum('sp,pab->sab', chosen.astype(jnp.bfloat16), patches...  12 us
    all_to_all x1, starting transfers between devices, exchange(): lax.all_to_all(labels, ('gx', 'gy'), split_axis=0, concat_axis=0, tiled=T...  11.5 us
    all_to_all x1, starting transfers between devices, exchange(): lax.all_to_all(outgoing, ('gx', 'gy'), split_axis=0, concat_axis=0, tiled...  10.2 us
    dot_general x1, matrix products, exchange(): jnp.einsum('sp,pab->sab', chosen.astype(jnp.bfloat16), patches, preferred...  9.51 us
    dot_general x1, matrix products, exchange(): jnp.einsum('sm,mab->sab', placing, arrived, preferred_element_type=jnp.fl...  7.85 us
  transfers between devices with their start and end apart: 2, of which 1 were waited for; matrix products, arithmetic and copies ran while one was open for 11% of the time, Pallas kernels for 0%

profile of v1, /device:TPU:1, one launch (start us, length us, event | category | flops | bytes accessed | tf_op | source)
XLA Modules:
  0.0 204.2 jit_solution(3724430146195811570)
XLA Ops:
  0.6 0.9 fusion.3
  1.5 0.7 convert_add_fusion
  2.2 0.7 convert_bitcast_fusion
  2.9 0.1 select_reduce_fusion
  3.0 0.8 convert_element_type.65
  3.8 11.5 %all-to-all-start = ((bf16[128,2,1]{1,2,0:T(2,128)(2,1)}), bf16[128,2,1]{1,2,0:T(2,128)(2,1)S(1)}, u32[]{:S(2)}, u32[]{:S(2)}) async-start(bf16[128,2,1]{1,2,0:T(2,128)(2,1)} %convert_element_type.65), calls=%async_computation | async-start | bytes 131072 | tf_op jit(solution)/shard_map/all_to_all | solution.py:361
  15.3 9.5 %convolution_convert_fusion = bf16[256,128,128]{2,0,1:T(8,128)(2,1)} fusion(bf16[128,128,128]{2,1,0:T(8,128)(2,1)} %param.11, s32[128]{0:T(128)S(1)} %convert_add_fusion), kind=kOutput, calls=%fused_computation.2 | convolution fusion | flops 1077968896 | bytes 12583424 | tf_op jit(solution)/shard_map/sp,pab->sab/dot_general | solution.py:353
  24.8 12.0 %copy.14 = bf16[256,128,128]{2,1,0:T(8,128)(2,1)} copy(bf16[256,128,128]{2,0,1:T(8,128)(2,1)} %convolution_convert_fusion) | data formatting | bytes 16777216 | tf_op jit(solution)/shard_map/convert_element_type | solution.py:355
  36.8 0.0 all-to-all-done
  36.8 10.2 %all-to-all-start.1 = ((bf16[256,128,128]{2,1,0:T(8,128)(2,1)}), bf16[256,128,128]{2,1,0:T(8,128)(2,1)}, u32[]{:S(2)}, u32[]{:S(2)}) async-start(bf16[256,128,128]{2,1,0:T(8,128)(2,1)} %copy.14), calls=%async_computation.1 | async-start | bytes 16777216 | tf_op jit(solution)/shard_map/all_to_all | solution.py:360
  47.0 0.0 copy-start
  47.1 0.0 copy-start.1
  47.1 0.0 copy-start.2
  47.1 0.2 convert_reduce_fusion
  47.3 0.1 reshape.51
  47.4 104.2 %all-to-all-done.1 = bf16[256,128,128]{2,1,0:T(8,128)(2,1)} async-done(((bf16[256,128,128]{2,1,0:T(8,128)(2,1)}), bf16[256,128,128]{2,1,0:T(8,128)(2,1)}, u32[]{:S(2)}, u32[]{:S(2)}) %all-to-all-start.1) | async-done | bytes 8388640 | tf_op jit(solution)/shard_map/all_to_all | solution.py:360
  151.6 7.9 %fusion = f32[2,128,128]{2,0,1:T(2,128)S(1)} fusion(bf16[256,128,128]{2,1,0:T(8,128)(2,1)} %all-to-all-done.1, f32[256]{0:T(256)S(1)} %reshape.51, f32[2]{0:T(128)S(1)} %add_convert_fusion), kind=kOutput, calls=%fused_computation | convolution fusion | flops 16777728 | bytes 8520712 | tf_op jit(solution)/shard_map/sm,mab->sab/dot_general | solution.py:367
  159.5 0.0 copy-done
  159.5 0.0 copy-done.1
  159.5 0.0 copy-done.2
  159.5 42.7 %shard_map.113 = (f32[8,128,256]{2,1,0:T(8,128)S(1)}, f32[8,128,256]{2,1,0:T(8,128)S(1)}) custom-call(f32[128,256]{1,0:T(8,128)S(1)} %bitcast.15, f32[8,128,256]{2,1,0:T(8,128)S(1)} %copy-done, f32[8,128,256]{2,1,0:T(8,128)S(1)} %copy-done.1, f32[8,128,256]{2,1,0:T(8,128)S(1)} %copy-done.2, f32[8,128,256]{2,1,0:T(8,128)} %refs_4_.1, f32[8,128,256]{2,1,0:T(8,128)} %refs_5_.1, ...), custom_call_target="tpu_custom_call" | custom-call | tf_op jit(solution)/shard_map/pallas_call | solution.py:313
  202.3 1.0 copy.25
  203.2 1.0 copy.26
  (2 shorter events, 0.0 us)
Async XLA Ops:
  3.8 33.0 %all-to-all-start = ((bf16[128,2,1]{1,2,0:T(2,128)(2,1)}), bf16[128,2,1]{1,2,0:T(2,128)(2,1)S(1)}, u32[]{:S(2)}, u32[]{:S(2)}) async-start(bf16[128,2,1]{1,2,0:T(2,128)(2,1)} %convert_element_type.65), calls=%async_computation | async-start | bytes 131072 | tf_op jit(solution)/shard_map/all_to_all | solution.py:361
  36.8 114.8 %all-to-all-start.1 = ((bf16[256,128,128]{2,1,0:T(8,128)(2,1)}), bf16[256,128,128]{2,1,0:T(8,128)(2,1)}, u32[]{:S(2)}, u32[]{:S(2)}) async-start(bf16[256,128,128]{2,1,0:T(8,128)(2,1)} %copy.14), calls=%async_computation.1 | async-start | bytes 16777216 | tf_op jit(solution)/shard_map/all_to_all | solution.py:360
  47.0 112.5 %copy-start = (f32[8,128,256]{2,1,0:T(8,128)S(1)}, f32[8,128,256]{2,1,0:T(8,128)}, u32[]{:S(2)}) copy-start(f32[8,128,256]{2,1,0:T(8,128)} %refs_1_.1) | copy-start | bytes 3145732
  47.1 112.5 %copy-start.1 = (f32[8,128,256]{2,1,0:T(8,128)S(1)}, f32[8,128,256]{2,1,0:T(8,128)}, u32[]{:S(2)}) copy-start(f32[8,128,256]{2,1,0:T(8,128)} %refs_2_.1) | copy-start | bytes 3145732
  47.1 112.5 %copy-start.2 = (f32[8,128,256]{2,1,0:T(8,128)S(1)}, f32[8,128,256]{2,1,0:T(8,128)}, u32[]{:S(2)}) copy-start(f32[8,128,256]{2,1,0:T(8,128)} %refs_3_.1) | copy-start | bytes 3145732

commit v2 on v1

--- a/solution.py
+++ b/solution.py
@@ -331,47 +331,226 @@
     )(*args)
 
 
-def exchange(patches, owners, slots, tile_cols):
-    count_x = lax.axis_size("gx")
-    count_y = lax.axis_size("gy")
-    devices_all = count_x * count_y
-    per_device = patches.shape[0]
+ORDERS = (("x", "y", "z"), ("y", "z", "x"), ("z", "x", "y"))
+DIMS = {"x": "zy", "y": "xz", "z": "xy"}
+
+
+def portions(side):
+    tiles = side // 16
+    cut = [0, -(-tiles // 3), -(-2 * tiles // 3), tiles]
+    return [(16 * cut[i], 16 * (cut[i + 1] - cut[i])) for i in range(3)]
+
+
+def exchange_body(
+    lay, cap, owners, slots, patches, surface, held, packed, arrived, summed, landed, second,
+    third, index_v, weight_v, weight_in, index_s, weight_s, load_sem, move_sem,
+    send1, recv1, send1w, recv1w, send2, recv2, send3, recv3,
+):
+    per_device, side, _ = patches.shape
+    me = dict(zip("xzcy", lay.me()))
+    count = dict(x=lay.nx, y=lay.ny, z=lay.nz)
+    parts = portions(side)
+    load = pltpu.make_async_copy(patches, held, load_sem.at[0])
+    load.start()
+
+    shape = (per_device, 128)
+    patch_ids = lax.broadcasted_iota(jnp.int32, shape, 0)
+    hit = jnp.broadcast_to(owners[...], shape) == lax.broadcasted_iota(jnp.int32, shape, 1)
+    slot = jnp.broadcast_to(slots[...], shape)
+    first = jnp.min(jnp.where(hit, patch_ids, per_device), axis=0, keepdims=True)
+    last = jnp.max(jnp.where(hit, patch_ids, -1), axis=0, keepdims=True)
+    index_v[0:1, :] = jnp.minimum(first, per_device - 1)
+    index_v[1:2, :] = jnp.maximum(last, 0)
+    for j in range(cap):
+        chosen = patch_ids == (first if j == 0 else last)
+        if j > 0:
+            chosen = jnp.logical_and(chosen, last > first)
+        chosen = jnp.logical_and(hit, chosen)
+        for s in range(2):
+            weight_v[2 * j + s : 2 * j + s + 1, :] = jnp.sum(
+                jnp.where(jnp.logical_and(chosen, slot == s), 1.0, 0.0), axis=0, keepdims=True
+            )
+    to_scalar = pltpu.make_async_copy(index_v, index_s, move_sem.at[0])
+    to_scalar.start()
+    own_weight = pltpu.make_async_copy(weight_v, weight_s.at[0, 0], move_sem.at[1])
+    own_weight.start()
+
+    offsets = [(d, c) for d in range(4) for c in range(lay.cores) if (d, c) != (0, 0)]
+
+    def moved(axis, d, c):
+        return lay.moved(**{"d" + axis: d, "dc": c})
+
+    weight_copies = []
+    for q, order in enumerate(ORDERS):
+        weight_copies.append([
+            remote(weight_v, weight_in.at[q, i], send1w.at[q, i], recv1w.at[q, i],
+                   moved(order[0], d, c))
+            for i, (d, c) in enumerate(offsets)
+        ])
+        for copy in weight_copies[-1]:
+            copy.start()
+
+    load.wait()
+    to_scalar.wait()
+    own_weight.wait()
+
+    def pack(o, carry):
+        for j in range(cap):
+            packed[o // 32, o // 8 % 4, o // 4 % 2, o % 4, j] = held[index_s[j, o]]
+        return carry
+
+    lax.fori_loop(0, 128, pack, 0)
+
+    def outgoing(q, a, c):
+        at = pl.ds(*parts[q])
+        axis = ORDERS[q][0]
+        if axis == "x":
+            return packed.at[a, :, c, :, :, at, :]
+        if axis == "y":
+            return packed.at[:, :, c, a, :, at, :]
+        return packed.at[:, a, c, :, :, at, :]
+
+    copies1 = []
+    for i, (d, c) in enumerate(offsets):
+        for q, order in enumerate(ORDERS):
+            axis = order[0]
+            copy = remote(
+                outgoing(q, (me[axis] + d) % 4, (me["c"] + c) % lay.cores),
+                arrived[q].at[i], send1.at[q, i], recv1.at[q, i], moved(axis, d, c),
+            )
+            copy.start()
+            copies1.append((q, copy))
+
+    copies2, copies3 = [], []
+    for q, order in enumerate(ORDERS):
+        for copy in weight_copies[q]:
+            copy.wait()
+        gather = pltpu.make_async_copy(weight_in.at[q], weight_s.at[q, pl.ds(1, 7)], move_sem.at[2 + q])
+        gather.start()
+        gather.wait()
+        for p, copy in copies1:
+            if p == q:
+                copy.wait()
+        at = pl.ds(*parts[q])
+        rows = parts[q][1]
+        dims = DIMS[order[0]]
+
+        def reduce(k, carry, q=q, order=order, at=at, rows=rows, dims=dims):
+            spot = {dims[0]: k // 4, dims[1]: k % 4, order[0]: me[order[0]]}
+            owner = spot["x"] * 32 + spot["z"] * 8 + me["c"] * 4 + spot["y"]
+            sums = [jnp.zeros((rows, side), jnp.float32) for _ in range(2)]
+            for source in range(8):
+                for j in range(cap):
+                    if source == 0:
+                        value = packed[spot["x"], spot["z"], me["c"], spot["y"], j, at, :]
+                    else:
+                        value = arrived[q][source - 1, k // 4, k % 4, j]
+                    value = value.astype(jnp.float32)
+                    table = (0, 0) if source == 0 else (q, source)
+                    for s in range(2):
+                        sums[s] = sums[s] + weight_s[(*table, 2 * j + s, owner)] * value
+            for s in range(2):
+                summed[q][spot[order[1]], spot[order[2]], s] = sums[s]
+            return carry
+
+        lax.fori_loop(0, 16, reduce, 0)
+        mine = []
+        for d in range(1, 4):
+            copy = remote(summed[q].at[(me[order[1]] + d) % 4], landed[q].at[d - 1],
+                          send2.at[q, d - 1], recv2.at[q, d - 1], moved(order[1], d, 0))
+            copy.start()
+            mine.append(copy)
+        copies2.append(mine)
+    for q, order in enumerate(ORDERS):
+        for copy in copies2[q]:
+            copy.wait()
+
+        def reduce(k, carry, q=q, order=order):
+            total = summed[q][me[order[1]], k]
+            for d in range(3):
+                total = total + landed[q][d, k]
+            second[q][k] = total
+            return carry
+
+        lax.fori_loop(0, 4, reduce, 0)
+        mine = []
+        for d in range(1, 4):
+            copy = remote(second[q].at[(me[order[2]] + d) % 4], third[q].at[d - 1],
+                          send3.at[q, d - 1], recv3.at[q, d - 1], moved(order[2], d, 0))
+            copy.start()
+            mine.append(copy)
+        copies3.append(mine)
+    for q, order in enumerate(ORDERS):
+        for copy in copies3[q]:
+            copy.wait()
+        for s in range(2):
+            total = second[q][me[order[2]], s]
+            for d in range(3):
+                total = total + third[q][d, s]
+            surface[pl.ds(*parts[q]), s * side : (s + 1) * side] = total
+
+
+def exchange_scratch(cap, side):
+    parts = portions(side)
+
+    def each(*lead, kind=jnp.float32):
+        return [pltpu.VMEM((*lead, rows, side), kind) for _, rows in parts]
+
+    bf16 = jnp.bfloat16
+    dma = pltpu.SemaphoreType.DMA
+    return [
+        pltpu.VMEM((128, side, side), bf16),
+        pltpu.VMEM((4, 4, 2, 4, cap, side, side), bf16),
+        each(7, 4, 4, cap, kind=bf16), each(4, 4, 2), each(3, 4, 2), each(4, 2), each(3, 2),
+        pltpu.VMEM((8, 128), jnp.int32), pltpu.VMEM((8, 128), jnp.float32),
+        pltpu.VMEM((3, 7, 8, 128), jnp.float32),
+        pltpu.SMEM((8, 128), jnp.int32), pltpu.SMEM((3, 8, 8, 128), jnp.float32),
+        dma((1,)), dma((5,)),
+        dma((3, 7)), dma((3, 7)), dma((3, 7)), dma((3, 7)),
+        dma((3, 3)), dma((3, 3)), dma((3, 3)), dma((3, 3)),
+    ]
+
+
+def exchange_friends(lay):
+    return [
+        lay.moved(**{"d" + axis: d, "dc": c})
+        for axis in "xyz" for d in range(4) for c in range(lay.cores) if (d, c) != (0, 0)
+    ]
+
+
+def meet(friends):
+    barrier = pltpu.get_barrier_semaphore()
+    for friend in friends:
+        pl.semaphore_signal(barrier, inc=1, device_id=friend, device_id_type=MESH)
+    pl.semaphore_wait(barrier, len(friends))
+
+
+def exchange_kernel(lay, cap, *refs):
+    meet(exchange_friends(lay))
+    exchange_body(lay, cap, *refs)
+
+
+def exchange(lay, cap, patches, owners, slots, tile_cols):
     side = patches.shape[1]
-    slot_count = tile_cols // side
-    owner_list = owners[:, 0]
-    slot_list = slots[:, 0]
-    targets = jnp.arange(devices_all, dtype=jnp.int32)
-    owner_hits = (owner_list[:, None] == targets[None, :]).astype(jnp.float32)
-    earlier = (jnp.arange(per_device)[:, None] > jnp.arange(per_device)[None, :]).astype(
-        jnp.float32
-    )
-    before = jnp.dot(earlier, owner_hits, precision=lax.Precision.HIGHEST)
-    ranking = jnp.sum(before * owner_hits, axis=1).astype(jnp.int32)
-    destination = owner_list * CAP + ranking
-    mailbox = jnp.arange(devices_all * CAP, dtype=jnp.int32)
-    chosen = mailbox[:, None] == destination[None, :]
-    outgoing = jnp.einsum(
-        "sp,pab->sab", chosen.astype(jnp.bfloat16), patches, preferred_element_type=jnp.float32
-    ).astype(jnp.bfloat16)
-    labels = jnp.sum(
-        chosen.astype(jnp.float32) * (slot_list + 1).astype(jnp.float32)[None, :], axis=1
-    ).astype(jnp.bfloat16)
-    arrived, arrived_labels = (
-        lax.all_to_all(outgoing, ("gx", "gy"), split_axis=0, concat_axis=0, tiled=True),
-        lax.all_to_all(labels, ("gx", "gy"), split_axis=0, concat_axis=0, tiled=True),
-    )
-    slot_ids = jnp.arange(1, slot_count + 1).astype(jnp.float32)
-    placing = (arrived_labels.astype(jnp.float32)[None, :] == slot_ids[:, None]).astype(
-        jnp.bfloat16
-    )
-    placed = jnp.einsum("sm,mab->sab", placing, arrived, preferred_element_type=jnp.float32)
-    return placed.transpose(1, 0, 2).reshape(side, slot_count * side)
+    return pl.pallas_call(
+        functools.partial(exchange_kernel, lay, cap),
+        out_shape=jax.ShapeDtypeStruct((side, tile_cols), jnp.float32),
+        in_specs=[
+            pl.BlockSpec(memory_space=pltpu.VMEM), pl.BlockSpec(memory_space=pltpu.VMEM),
+            pl.BlockSpec(memory_space=pl.ANY),
+        ],
+        out_specs=pl.BlockSpec(memory_space=pltpu.VMEM),
+        scratch_shapes=exchange_scratch(cap, side),
+        compiler_params=pltpu.CompilerParams(
+            collective_id=2, has_side_effects=True, vmem_limit_bytes=48 * MIB
+        ),
+    )(owners, slots, patches)
 
 
 def on_device(forcing, patches, owners, slots, cond_x, cond_y, cond_z, storage, fixed, closed):
     count_x, count_y = lax.axis_size("gx"), lax.axis_size("gy")
     lay = Layout(count_x, count_y)
-    surface = exchange(patches, owners, slots, forcing.shape[2])
+    surface = exchange(lay, CAP, patches, owners, slots, forcing.shape[2])
     return tuple(
         cg(lay, count_x, count_y, surface, forcing, cond_x, cond_y, cond_z, storage, fixed, closed)
     )

time: 205 us -> 120 us (0.59)
  waiting for transfers between devices: 104 us -> 0 us
  Pallas kernels: 42.7 us -> 112 us
  starting transfers between devices: 21.7 us -> 0 us
  matrix products: 18.3 us -> 0 us
  local copies, waits for them, and re-layouts: 14.9 us -> 5.66 us
    all_to_all x2 -> x0, waiting for transfers between devices: 104 us -> none  [the longest x1 104 us: exchange(): lax.all_to_all(outgoing, ('gx', 'gy'), split_axis=0, concat_axis=0, tiled...]
    pallas_call x0 -> x1, Pallas kernels: none -> 68.2 us  [exchange(): pl.pallas_call(functools.partial(exchange_kernel, lay, cap), out_shape=ja...]
    all_to_all x2 -> x0, starting transfers between devices: 21.7 us -> none  [the longest x1 11.5 us: exchange(): lax.all_to_all(labels, ('gx', 'gy'), split_axis=0, concat_axis=0, tiled=T...]
    dot_general x3 -> x0, matrix products: 18.3 us -> none  [the longest x1 9.51 us: exchange(): jnp.einsum('sp,pab->sab', chosen.astype(jnp.bfloat16), patches, preferred...]
    convert_element_type x3 -> x0, local copies, waits for them, and re-layouts: 12.9 us -> none  [the longest x1 12 us: exchange(): outgoing = jnp.einsum('sp,pab->sab', chosen.astype(jnp.bfloat16), patches...]
    unnamed x9 -> x12, local copies, waits for them, and re-layouts: 1.97 us -> 5.66 us
  transfers between devices with their start and end apart: 2 -> 0, of which waited for: 1 -> 0; matrix products, arithmetic and copies ran while one was open for 11% -> 0% of each run, Pallas kernels for 0% -> 0%
where the time goes in v2:
time: 120 us; the launch traced here: 118 us
  Pallas kernels  112 us (93%)
  local copies, waits for them, and re-layouts  5.66 us (5%)
    pallas_call x1, Pallas kernels, exchange(): pl.pallas_call(functools.partial(exchange_kernel, lay, cap), out_shape=ja...  68.2 us
    pallas_call x1, Pallas kernels, cg(): pl.pallas_call(functools.partial(cg_kernel, lay, count_x, count_y), out_s...  43.8 us
    unnamed x12, local copies, waits for them, and re-layouts  5.66 us

profile of v2, /device:TPU:1, one launch (start us, length us, event | category | flops | bytes accessed | tf_op | source)
XLA Modules:
  0.0 118.3 jit_solution(2764435233021540064)
XLA Ops:
  0.6 0.8 copy.12.refs_0_
  1.4 0.8 copy.13.refs_1_
  2.2 0.0 copy-start
  2.2 2.2 %copy-done = bf16[128,128,128]{2,1,0:T(8,128)(2,1)S(1)} copy-done((bf16[128,128,128]{2,1,0:T(8,128)(2,1)S(1)}, bf16[128,128,128]{2,1,0:T(8,128)(2,1)}, u32[]{:S(2)}) %copy-start) | copy-done | bytes 4194328
  4.3 0.0 copy-start.1
  4.3 0.0 copy-start.2
  4.3 0.0 copy-start.3
  4.3 68.2 %shard_map.113.refs_0_ = f32[128,256]{1,0:T(8,128)S(1)} custom-call(s32[128,1]{1,0:T(8,128)S(1)} %copy.12.refs_0_, s32[128,1]{1,0:T(8,128)S(1)} %copy.13.refs_1_, bf16[128,128,128]{2,1,0:T(8,128)(2,1)S(1)} %copy-done), custom_call_target="tpu_custom_call" | custom-call | tf_op jit(solution)/shard_map/pallas_call | solution.py:535
  72.6 0.0 copy-done.1
  72.6 0.0 copy-done.2
  72.6 0.0 copy-done.3
  72.6 43.8 %shard_map.114 = (f32[8,128,256]{2,1,0:T(8,128)S(1)}, f32[8,128,256]{2,1,0:T(8,128)S(1)}) custom-call(f32[128,256]{1,0:T(8,128)S(1)} %shard_map.113.refs_0_, f32[8,128,256]{2,1,0:T(8,128)S(1)} %copy-done.1, f32[8,128,256]{2,1,0:T(8,128)S(1)} %copy-done.2, f32[8,128,256]{2,1,0:T(8,128)S(1)} %copy-done.3, f32[8,128,256]{2,1,0:T(8,128)} %refs_4_.1, ...), custom_call_target="tpu_custom_call" | custom-call | tf_op jit(solution)/shard_map/pallas_call | solution.py:313
  116.4 1.0 copy.16
  117.4 1.0 copy.17
Async XLA Ops:
  2.2 2.2 %copy-start = (bf16[128,128,128]{2,1,0:T(8,128)(2,1)S(1)}, bf16[128,128,128]{2,1,0:T(8,128)(2,1)}, u32[]{:S(2)}) copy-start(bf16[128,128,128]{2,1,0:T(8,128)(2,1)} %refs_2_.2) | copy-start | bytes 12582916
  4.3 68.3 %copy-start.1 = (f32[8,128,256]{2,1,0:T(8,128)S(1)}, f32[8,128,256]{2,1,0:T(8,128)}, u32[]{:S(2)}) copy-start(f32[8,128,256]{2,1,0:T(8,128)} %refs_1_.2) | copy-start | bytes 3145732
  4.3 68.3 %copy-start.2 = (f32[8,128,256]{2,1,0:T(8,128)S(1)}, f32[8,128,256]{2,1,0:T(8,128)}, u32[]{:S(2)}) copy-start(f32[8,128,256]{2,1,0:T(8,128)} %refs_2_.3) | copy-start | bytes 3145732
  4.3 68.3 %copy-start.3 = (f32[8,128,256]{2,1,0:T(8,128)S(1)}, f32[8,128,256]{2,1,0:T(8,128)}, u32[]{:S(2)}) copy-start(f32[8,128,256]{2,1,0:T(8,128)} %refs_3_.1) | copy-start | bytes 3145732

commit v3 on v2

v3 whole, which is shorter than its diff:
```python
import functools

import jax
import jax.numpy as jnp
from jax import lax
from jax.experimental import pallas as pl
from jax.experimental.pallas import tpu as pltpu
from jax.sharding import PartitionSpec as P

MESH = pl.DeviceIdType.MESH
PAD = 8
MIB = 1 << 20


class Layout:
    def __init__(self, count_x, count_y):
        self.cores = 2 if count_x % 2 == 0 else 1
        chips = count_x // self.cores
        self.nz = 4 if chips % 4 == 0 else chips
        self.nx = chips // self.nz
        self.ny = count_y

    def me(self):
        gx, gy = lax.axis_index("gx"), lax.axis_index("gy")
        core = gx % self.cores
        chip = gx // self.cores
        return chip // self.nz, chip % self.nz, core, gy

    def device(self, x, z, core, y):
        return ((x * self.nz + z) * self.cores + core, y)

    def moved(self, dx=0, dz=0, dc=0, dy=0):
        x, z, core, y = self.me()
        return self.device(
            (x + dx) % self.nx, (z + dz) % self.nz, (core + dc) % self.cores, (y + dy) % self.ny
        )

    def stages(self):
        first = [
            dict(dc=c, dy=y) for c in range(self.cores) for y in range(self.ny) if (c, y) != (0, 0)
        ]
        second = [
            dict(dx=x, dz=z) for x in range(self.nx) for z in range(self.nz) if (x, z) != (0, 0)
        ]
        return [first, second]


def remote(src, dst, send, recv, device):
    return pltpu.make_async_remote_copy(
        src_ref=src, dst_ref=dst, send_sem=send, recv_sem=recv, device_id=device, device_id_type=MESH
    )


class Solve:
    names = (
        "forcing", "cond_x", "cond_y", "cond_z", "storage", "fixed", "closed", "tees", "east",
        "north", "south", "above", "inverse", "enns", "col_out", "col_in", "partial", "gathered",
        "halo_send", "halo_recv", "sum_send", "sum_recv",
    )

    def __init__(self, lay, count_x, count_y, refs):
        self.lay, self.count_x, self.count_y = lay, count_x, count_y
        for name, ref in zip(self.names, refs, strict=True):
            setattr(self, name, ref)
        self.layers, self.rows, self.cols = self.forcing.shape
        self.step = 32
        self.blocks = self.rows // self.step
        gx, gy = lax.axis_index("gx"), lax.axis_index("gy")
        self.gx, self.gy = gx, gy
        self.right = ((gx + 1) % count_x, gy)
        self.left = ((gx + count_x - 1) % count_x, gy)
        self.up = (gx, (gy + 1) % count_y)
        self.down = (gx, (gy + count_y - 1) % count_y)
        lanes = lax.broadcasted_iota(jnp.int32, (self.step, self.cols), 1)
        self.first_lane, self.last_lane = lanes == 0, lanes == self.cols - 1
        square = (self.rows, self.rows)
        self.eye = lax.broadcasted_iota(jnp.int32, square, 0) == lax.broadcasted_iota(
            jnp.int32, square, 1
        )
        self.zero = jnp.zeros((8, self.cols), jnp.float32)
        self.moments = [self.zero] * 6

    def load_faces(self):
        for i in (1, 6, 2, 3):
            self.loads[i].wait()

    def load_rest(self):
        for i in (4, 5, 0):
            self.loads[i].wait()

    def column(self, block):
        wide = jnp.broadcast_to(block, (self.rows, self.rows))
        return jnp.sum(jnp.where(self.eye, wide, 0.0), axis=0, keepdims=True)

    def uncolumn(self, row, block):
        wide = jnp.broadcast_to(row, (self.step, self.rows))
        mask = self.eye[block * self.step : (block + 1) * self.step]
        return jnp.sum(jnp.where(mask, wide, 0.0), axis=1, keepdims=True)

    def fold(self, x):
        parts = [x[i * 8 : (i + 1) * 8] for i in range(self.step // 8)]
        while len(parts) > 1:
            parts = [a + b for a, b in zip(parts[::2], parts[1::2])]
        return parts[0]

    def faces(self):
        layers, rows, cols, step = self.layers, self.rows, self.cols, self.step
        east_last = jnp.where(self.gx == self.count_x - 1, 0.0, 1.0).astype(jnp.float32)
        north_last = jnp.where(self.gy == self.count_y - 1, 0.0, 1.0).astype(jnp.float32)
        north_scale = jnp.where(self.last_lane, north_last, 1.0)
        row_ids = lax.broadcasted_iota(jnp.int32, (step, cols), 0)

        def body(layer, carry):
            for b in range(self.blocks):
                at = pl.ds(b * step, step)
                open_faces = (1 - self.closed[layer, at, :]).astype(jnp.float32)
                scale = jnp.where(row_ids == rows - 1 - b * step, east_last, 1.0)
                self.east[layer, pl.ds(PAD + b * step, step), :] = (
                    self.cond_x[layer, at, :] * open_faces * scale
                )
                self.north[layer, at, :] = self.cond_y[layer, at, :] * open_faces * north_scale
            self.above[layer + 1] = self.cond_z[layer] * jnp.where(layer == layers - 1, 0.0, 1.0)
            self.col_out[0, 0, pl.ds(layer, 1), :] = self.column(
                self.north[layer, :, cols - 1 : cols]
            )
            return carry

        self.above[0] = jnp.zeros((rows, cols), jnp.float32)
        lax.fori_loop(0, layers, body, 0)
        self.rims = [
            remote(self.east.at[:, pl.ds(PAD + rows - 1, 1), :],
                   self.east.at[:, pl.ds(PAD - 1, 1), :],
                   self.halo_send.at[0, 0], self.halo_recv.at[0, 0], self.right),
            remote(self.col_out.at[0, 0], self.col_in.at[0, 0],
                   self.halo_send.at[0, 1], self.halo_recv.at[0, 1], self.up),
        ]

    def send_rims(self):
        for copy in self.rims:
            copy.start()

    def prepare(self):
        step = self.step
        for copy in self.rims:
            copy.wait()

        def body(layer, carry):
            south_row = self.col_in[0, 0, pl.ds(layer, 1), :]
            for b in range(self.blocks):
                at = pl.ds(b * step, step)
                north = self.north[layer, at, :]
                south = jnp.where(
                    self.first_lane, self.uncolumn(south_row, b), pltpu.roll(north, 1, 1)
                )
                self.south[layer, at, :] = south
                keep = (1 - self.fixed[layer, at, :]).astype(jnp.float32)
                diagonal = (
                    self.storage[layer, at, :]
                    + self.east[layer, pl.ds(PAD + b * step, step), :]
                    + self.east[layer, pl.ds(PAD - 1 + b * step, step), :]
                    + north + south + self.above[layer + 1, at, :] + self.above[layer, at, :]
                )
                self.inverse[layer, at, :] = keep / diagonal
            return carry

        lax.fori_loop(0, self.layers, body, 0)

    def start(self, low, high, surface=None):
        step = self.step

        def body(layer, total):
            for b in range(self.blocks):
                at = pl.ds(b * step, step)
                keep = (1 - self.fixed[layer, at, :]).astype(jnp.float32)
                value = self.forcing[layer, at, :]
                if surface is not None:
                    value = value + surface[at, :]
                value = keep * value
                self.enns[0, layer, at, :] = value
                tee = self.inverse[layer, at, :] * value
                self.tees[0, layer, pl.ds(PAD + b * step, step), :] = tee
                total = total + self.fold(tee * value)
            return total

        self.moments[0] = lax.fori_loop(low, high, body, self.moments[0])

    def send(self, j, low, high, early):
        rows, cols = self.rows, self.cols

        def body(layer, carry):
            here = self.tees.at[j, layer, pl.ds(PAD, rows), :]
            self.col_out[j + 1, 0, pl.ds(layer, 1), :] = self.column(here[:, cols - 1 : cols])
            self.col_out[j + 1, 1, pl.ds(layer, 1), :] = self.column(here[:, 0:1])
            return carry

        lax.fori_loop(low, high, body, 0)
        some = pl.ds(low, high - low)
        tee = self.tees.at[j, some]
        k = 2 * j + 1 + early
        copies = [
            remote(tee.at[:, pl.ds(PAD + rows - 1, 1), :], tee.at[:, pl.ds(PAD - 1, 1), :],
                   self.halo_send.at[k, 0], self.halo_recv.at[k, 0], self.right),
            remote(tee.at[:, pl.ds(PAD, 1), :], tee.at[:, pl.ds(PAD + rows, 1), :],
                   self.halo_send.at[k, 1], self.halo_recv.at[k, 1], self.left),
            remote(self.col_out.at[j + 1, 0, some], self.col_in.at[j + 1, 0, some],
                   self.halo_send.at[k, 2], self.halo_recv.at[k, 2], self.up),
            remote(self.col_out.at[j + 1, 1, some], self.col_in.at[j + 1, 1, some],
                   self.halo_send.at[k, 3], self.halo_recv.at[k, 3], self.down),
        ]
        for copy in copies:
            copy.start()
        return copies

    def apply(self, j, low, high):
        layers, cols, step, tees = self.layers, self.cols, self.step, self.tees

        def body(layer, carry):
            odd, even = carry
            south_row = self.col_in[j + 1, 0, pl.ds(layer, 1), :]
            north_row = self.col_in[j + 1, 1, pl.ds(layer, 1), :]
            higher = jnp.minimum(layer + 1, layers - 1)
            lower = jnp.maximum(layer - 1, 0)
            for b in range(self.blocks):
                at = pl.ds(b * step, step)
                mid = pl.ds(PAD + b * step, step)
                before = pl.ds(PAD - 1 + b * step, step)
                after = pl.ds(PAD + 1 + b * step, step)
                here = tees[j, layer, mid, :]
                north = jnp.where(
                    self.last_lane, self.uncolumn(north_row, b), pltpu.roll(here, cols - 1, 1)
                )
                south = jnp.where(
                    self.first_lane, self.uncolumn(south_row, b), pltpu.roll(here, 1, 1)
                )
                flux = self.east[layer, mid, :] * tees[j, layer, after, :]
                flux += self.east[layer, before, :] * tees[j, layer, before, :]
                flux += self.north[layer, at, :] * north + self.south[layer, at, :] * south
                flux += self.above[layer + 1, at, :] * tees[j, higher, mid, :]
                flux += self.above[layer, at, :] * tees[j, lower, mid, :]
                self.enns[j + 1, layer, at, :] = flux
                odd = odd + self.fold(here * flux)
                if j < 2:
                    tee = self.inverse[layer, at, :] * flux
                    tees[j + 1, layer, mid, :] = tee
                    even = even + self.fold(tee * flux)
            return odd, even

        last = self.moments[2 * j + 2] if j < 2 else self.zero
        odd, even = lax.fori_loop(low, high, body, (self.moments[2 * j + 1], last))
        self.moments[2 * j + 1] = odd
        if j < 2:
            self.moments[2 * j + 2] = even

    def total(self, extra):
        partial, gathered = self.partial, self.gathered
        partial[0] = jnp.zeros((8, 128), jnp.float32)
        for k, value in enumerate(self.moments):
            both = sum(value[:, i * 128 : (i + 1) * 128] for i in range(self.cols // 128))
            partial[0, k : k + 1, :] = jnp.sum(both, axis=0, keepdims=True)
        partial[0, 6:7, :] = extra
        base = 0
        for s, peers in enumerate(self.lay.stages()):
            copies = [
                remote(partial.at[s], gathered.at[base + i], self.sum_send.at[base + i],
                       self.sum_recv.at[base + i], self.lay.moved(**offset))
                for i, offset in enumerate(peers)
            ]
            for copy in copies:
                copy.start()
            for copy in copies:
                copy.wait()
            total = partial[s]
            for i in range(len(peers)):
                total = total + gathered[base + i]
            base += len(peers)
            partial[s + 1] = total
        return partial[len(self.lay.stages())]

    def finish(self, total, solution, residual):
        sol_w, res_w = scalars(total)
        step = self.step

        def body(layer, carry):
            for b in range(self.blocks):
                at = pl.ds(b * step, step)
                mid = pl.ds(PAD + b * step, step)
                keep = (1 - self.fixed[layer, at, :]).astype(jnp.float32)
                out = sol_w[0] * self.tees[0, layer, mid, :]
                for j in range(1, 3):
                    out += sol_w[j] * self.tees[j, layer, mid, :]
                solution[layer, at, :] = out
                out = res_w[0] * self.enns[0, layer, at, :]
                for j in range(1, 4):
                    out += res_w[j] * self.enns[j, layer, at, :]
                residual[layer, at, :] = keep * out
            return carry

        lax.fori_loop(0, self.layers, body, 0)


def solve_scratch(lay, layers, rows, cols):
    peers = sum(len(s) for s in lay.stages())
    f32, dma = jnp.float32, pltpu.SemaphoreType.DMA

    def full(*lead, kind=f32):
        return pltpu.VMEM((*lead, layers, rows, cols), kind)

    def padded(*lead):
        return pltpu.VMEM((*lead, layers, rows + 2 * PAD, cols), f32)

    return [
        full(), full(), full(), full(), full(), full(kind=jnp.int32), full(kind=jnp.int32),
        padded(3), padded(), full(), full(),
        pltpu.VMEM((layers + 1, rows, cols), f32), full(), full(4),
        pltpu.VMEM((4, 2, layers, rows), f32), pltpu.VMEM((4, 2, layers, rows), f32),
        pltpu.VMEM((len(lay.stages()) + 1, 8, 128), f32), pltpu.VMEM((peers, 8, 128), f32),
        dma((7, 4)), dma((7, 4)), dma((peers,)), dma((peers,)),
    ]


def solve_friends(lay, count_x, count_y):
    gx, gy = lax.axis_index("gx"), lax.axis_index("gy")
    friends = [((gx + 1) % count_x, gy), ((gx + count_x - 1) % count_x, gy),
               (gx, (gy + 1) % count_y), (gx, (gy + count_y - 1) % count_y)]
    for peers in lay.stages():
        friends += [lay.moved(**offset) for offset in peers]
    return friends


def scalars(total):
    def reduce(row):
        return jnp.sum(row, axis=1, keepdims=True)

    rows = [total[k : k + 1, :] for k in range(6)]
    m0, m1 = reduce(rows[0]), reduce(rows[1])
    shift = jnp.where(m1 > 0.5 * m0, 1.0, 0.0)
    scale = 1.0 - shift
    c, current = [m0], rows
    for _ in range(5):
        current = [current[q + 1] - shift * current[q] for q in range(len(current) - 1)]
        c.append(reduce(current[0]))
    d = [scale * c[k] - c[k + 1] for k in range(5)]
    zero = jnp.zeros_like(m0)
    rho, pi, sol = [zero + 1.0], [zero + 1.0], [zero, zero, zero]
    inner = m0
    for i in range(3):
        curve = zero
        for a in range(len(pi)):
            for b in range(len(pi)):
                curve = curve + pi[a] * pi[b] * d[a + b]
        alpha = inner / curve
        for a in range(len(pi)):
            sol[a] = sol[a] + alpha * pi[a]
        rho = rho + [zero]
        for a in range(len(pi)):
            rho[a] = rho[a] - alpha * scale * pi[a]
            rho[a + 1] = rho[a + 1] + alpha * pi[a]
        if i < 2:
            inner_next = zero
            for a in range(len(rho)):
                for b in range(len(rho)):
                    inner_next = inner_next + rho[a] * rho[b] * c[a + b]
            beta = inner_next / inner
            pi = [rho[a] + beta * pi[a] if a < len(pi) else rho[a] for a in range(len(rho))]
            inner = inner_next

    def unshift(w):
        out = [zero] * len(w)
        for k in reversed(range(len(w))):
            moved = [zero] + out[:-1]
            out = [moved[i] - shift * out[i] for i in range(len(w))]
            out[0] = out[0] + w[k]
        return out

    return unshift(sol), unshift(rho)


ORDERS = (("x", "y", "z"), ("y", "z", "x"), ("z", "x", "y"))
DIMS = {"x": "zy", "y": "xz", "z": "xy"}


def portions(side):
    tiles = side // 16
    cut = [0, -(-tiles // 3), -(-2 * tiles // 3), tiles]
    return [(16 * cut[i], 16 * (cut[i + 1] - cut[i])) for i in range(3)]


def exchange_body(
    lay, cap, solve, enter, load, places, surface, held, packed, arrived, summed, landed, second,
    third, index_v, weight_v, weight_in, index_s, weight_s, move_sem,
    send1, recv1, send1w, recv1w, send2, recv2, send3, recv3, *star,
):
    per_device, side, _ = held.shape
    me = dict(zip("xzcy", lay.me()))
    count = dict(x=lay.nx, y=lay.ny, z=lay.nz)
    parts = portions(side)

    shape = (per_device, 128)
    patch_ids = lax.broadcasted_iota(jnp.int32, shape, 0)
    place = jnp.broadcast_to(places[...], shape) - 2 * lax.broadcasted_iota(jnp.int32, shape, 1)
    hit = jnp.logical_or(place == 0, place == 1)
    first = jnp.min(jnp.where(hit, patch_ids, per_device), axis=0, keepdims=True)
    last = jnp.max(jnp.where(hit, patch_ids, -1), axis=0, keepdims=True)
    index_v[0:1, :] = jnp.minimum(first, per_device - 1)
    index_v[1:2, :] = jnp.maximum(last, 0)
    again = last > first
    for j in range(2):
        chosen = patch_ids == (first if j == 0 else last)
        if j > 0:
            chosen = jnp.logical_and(chosen, again)
        chosen = jnp.logical_and(hit, chosen)
        for s in range(2):
            weight_v[2 * j + s : 2 * j + s + 1, :] = jnp.sum(
                jnp.where(jnp.logical_and(chosen, place == s), 1.0, 0.0), axis=0, keepdims=True
            )
    doubled = jnp.where(again, 1.0, 0.0)
    for s in range(2):
        weight_v[4 + s : 5 + s, :] = jnp.broadcast_to(
            jnp.sum(weight_v[2 + s : 3 + s, :], axis=1, keepdims=True), (1, 128)
        )
    extra = jnp.maximum(jnp.sum(doubled, axis=1, keepdims=True) - 1.0, 0.0)
    weight_v[6:7, :] = jnp.broadcast_to(extra, (1, 128))
    weight_v[7:8, :] = doubled
    spare_index = jnp.max(jnp.where(again, last, 0), axis=1, keepdims=True)
    index_v[2:3, :] = jnp.broadcast_to(spare_index, (1, 128))
    to_scalar = pltpu.make_async_copy(index_v, index_s, move_sem.at[0])
    to_scalar.start()
    own_weight = pltpu.make_async_copy(weight_v, weight_s.at[0, 0], move_sem.at[1])
    own_weight.start()

    offsets = [(d, c) for d in range(4) for c in range(lay.cores) if (d, c) != (0, 0)]

    def moved(axis, d, c):
        return lay.moved(**{"d" + axis: d, "dc": c})

    solve.load_faces()
    solve.faces()
    load.wait()
    to_scalar.wait()
    own_weight.wait()

    def pack(o, carry):
        for j in range(cap):
            packed[o // 32, o // 8 % 4, o // 4 % 2, o % 4, j] = held[index_s[j, o]]
        return carry

    lax.fori_loop(0, 128, pack, 0)
    common = Common(lay, me, held, weight_v, weight_in, *star) if cap == 1 else None
    if common:
        common.pack(index_s[2, 0])
    enter()
    solve.send_rims()
    if common:
        common.scatter()
    weight_copies = []
    for q, order in enumerate(ORDERS):
        weight_copies.append([
            remote(weight_v, weight_in.at[q, i], send1w.at[q, i], recv1w.at[q, i],
                   moved(order[0], d, c))
            for i, (d, c) in enumerate(offsets)
        ])
        for copy in weight_copies[-1]:
            copy.start()


    def outgoing(q, a, c):
        at = pl.ds(*parts[q])
        axis = ORDERS[q][0]
        if axis == "x":
            return packed.at[a, :, c, :, :, at, :]
        if axis == "y":
            return packed.at[:, :, c, a, :, at, :]
        return packed.at[:, a, c, :, :, at, :]

    copies1 = []
    for i, (d, c) in enumerate(offsets):
        for q, order in enumerate(ORDERS):
            axis = order[0]
            copy = remote(
                outgoing(q, (me[axis] + d) % 4, (me["c"] + c) % lay.cores),
                arrived[q].at[i], send1.at[q, i], recv1.at[q, i], moved(axis, d, c),
            )
            copy.start()
            copies1.append((q, copy))

    solve.load_rest()
    solve.prepare()
    solve.start(1, solve.layers)
    early = solve.send(0, 1, solve.layers, True)
    for copy in weight_copies[1]:
        copy.wait()
    if common:
        common.reduce()
    copies2, copies3 = [], []
    for q, order in enumerate(ORDERS):
        for copy in weight_copies[q]:
            if q != 1:
                copy.wait()
        gather = pltpu.make_async_copy(weight_in.at[q], weight_s.at[q, pl.ds(1, 7)], move_sem.at[2 + q])
        gather.start()
        gather.wait()
        for p, copy in copies1:
            if p == q:
                copy.wait()
        at = pl.ds(*parts[q])
        rows = parts[q][1]
        dims = DIMS[order[0]]

        def reduce(k, carry, q=q, order=order, at=at, rows=rows, dims=dims):
            spot = {dims[0]: k // 4, dims[1]: k % 4, order[0]: me[order[0]]}
            owner = spot["x"] * 32 + spot["z"] * 8 + me["c"] * 4 + spot["y"]
            sums = [jnp.zeros((rows, side), jnp.float32) for _ in range(2)]
            for source in range(8):
                for j in range(cap):
                    if source == 0:
                        value = packed[spot["x"], spot["z"], me["c"], spot["y"], j, at, :]
                    else:
                        value = arrived[q][source - 1, k // 4, k % 4, j]
                    value = value.astype(jnp.float32)
                    table = (0, 0) if source == 0 else (q, source)
                    for s in range(2):
                        sums[s] = sums[s] + weight_s[(*table, 2 * j + s, owner)] * value
            for s in range(2):
                summed[q][spot[order[1]], spot[order[2]], s] = sums[s]
            return carry

        lax.fori_loop(0, 16, reduce, 0)
        mine = []
        for d in range(1, 4):
            copy = remote(summed[q].at[(me[order[1]] + d) % 4], landed[q].at[d - 1],
                          send2.at[q, d - 1], recv2.at[q, d - 1], moved(order[1], d, 0))
            copy.start()
            mine.append(copy)
        copies2.append(mine)
    for copy in early:
        copy.wait()
    solve.apply(0, 2, solve.layers)
    early = solve.send(1, 2, solve.layers, True)
    if common:
        common.gather()
    for q, order in enumerate(ORDERS):
        for copy in copies2[q]:
            copy.wait()

        def reduce(k, carry, q=q, order=order):
            total = summed[q][me[order[1]], k]
            for d in range(3):
                total = total + landed[q][d, k]
            second[q][k] = total
            return carry

        lax.fori_loop(0, 4, reduce, 0)
        mine = []
        for d in range(1, 4):
            copy = remote(second[q].at[(me[order[2]] + d) % 4], third[q].at[d - 1],
                          send3.at[q, d - 1], recv3.at[q, d - 1], moved(order[2], d, 0))
            copy.start()
            mine.append(copy)
        copies3.append(mine)
    for copy in early:
        copy.wait()
    solve.apply(1, 3, solve.layers)
    early = solve.send(2, 3, solve.layers, True)
    for q, order in enumerate(ORDERS):
        for copy in copies3[q]:
            copy.wait()
        for s in range(2):
            total = second[q][me[order[2]], s]
            for d in range(3):
                total = total + third[q][d, s]
            surface[pl.ds(*parts[q]), s * side : (s + 1) * side] = total
    if common:
        common.add(surface)
    return early


class Common:
    def __init__(self, lay, me, held, weight_v, weight_in, spare, pieces, sums, others, whole,
                 send_a, recv_a, send_b, recv_b, send_c, recv_c):
        self.__dict__.update(locals())
        self.offsets = [(d, c) for d in range(4) for c in range(2) if (d, c) != (0, 0)]
        self.wide = lay.stages()[1]

    def piece(self, d, c):
        return (self.me["y"] + d) % 4 * 2 + (self.me["c"] + c) % 2

    def pack(self, index):
        for k in range(8):
            self.spare[k] = self.held[index, 16 * k : 16 * (k + 1), :]

    def scatter(self):
        self.copies = [
            remote(self.spare.at[self.piece(d, c)], self.pieces.at[i], self.send_a.at[i],
                   self.recv_a.at[i], self.lay.moved(dy=d, dc=c))
            for i, (d, c) in enumerate(self.offsets)
        ]
        for copy in self.copies:
            copy.start()

    def reduce(self):
        for copy in self.copies:
            copy.wait()
        for s in range(2):
            mine = self.spare[self.piece(0, 0)].astype(jnp.float32)
            total = self.weight_v[4 + s : 5 + s, :] * mine
            for i in range(7):
                weight = self.weight_in[1, i, 4 + s : 5 + s, :]
                total = total + weight * self.pieces[i].astype(jnp.float32)
            self.sums[0, s] = total
        self.copies = [
            remote(self.sums.at[0], self.others.at[i], self.send_b.at[i], self.recv_b.at[i],
                   self.lay.moved(**offset))
            for i, offset in enumerate(self.wide)
        ]
        for copy in self.copies:
            copy.start()

    def gather(self):
        for copy in self.copies:
            copy.wait()
        for s in range(2):
            total = self.sums[0, s]
            for i in range(len(self.wide)):
                total = total + self.others[i, s]
            self.sums[1, s] = total
        k = self.piece(0, 0)
        self.whole[k] = self.sums[1]
        self.copies = [
            remote(self.sums.at[1], self.whole.at[k], self.send_c.at[i], self.recv_c.at[i],
                   self.lay.moved(dy=d, dc=c))
            for i, (d, c) in enumerate(self.offsets)
        ]
        for copy in self.copies:
            copy.start()

    def add(self, surface):
        for copy in self.copies:
            copy.wait()
        me = self.me
        owner = me["x"] * 32 + me["z"] * 8 + me["c"] * 4 + me["y"]
        here = lax.broadcasted_iota(jnp.int32, (1, 128), 1) == owner
        mine = jnp.sum(jnp.where(here, self.weight_v[7:8, :], 0.0), axis=1, keepdims=True)
        for k in range(8):
            for s in range(2):
                at = (slice(16 * k, 16 * (k + 1)), slice(128 * s, 128 * (s + 1)))
                surface[at] = surface[at] + mine * self.whole[k, s]


def exchange_scratch(cap, side):
    parts = portions(side)

    def each(*lead, kind=jnp.float32):
        return [pltpu.VMEM((*lead, rows, side), kind) for _, rows in parts]

    bf16 = jnp.bfloat16
    dma = pltpu.SemaphoreType.DMA
    return [
        pltpu.VMEM((128, side, side), bf16),
        pltpu.VMEM((4, 4, 2, 4, cap, side, side), bf16),
        each(7, 4, 4, cap, kind=bf16), each(4, 4, 2), each(3, 4, 2), each(4, 2), each(3, 2),
        pltpu.VMEM((8, 128), jnp.int32), pltpu.VMEM((8, 128), jnp.float32),
        pltpu.VMEM((3, 7, 8, 128), jnp.float32),
        pltpu.SMEM((8, 128), jnp.int32), pltpu.SMEM((3, 8, 8, 128), jnp.float32),
        dma((5,)),
        dma((3, 7)), dma((3, 7)), dma((3, 7)), dma((3, 7)),
        dma((3, 3)), dma((3, 3)), dma((3, 3)), dma((3, 3)),
    ] + ([
        pltpu.VMEM((8, 16, side), bf16), pltpu.VMEM((7, 16, side), bf16),
        pltpu.VMEM((2, 2, 16, side), jnp.float32), pltpu.VMEM((15, 2, 16, side), jnp.float32),
        pltpu.VMEM((8, 2, 16, side), jnp.float32),
        dma((7,)), dma((7,)), dma((15,)), dma((15,)), dma((7,)), dma((7,)),
    ] if cap == 1 else [])


def exchange_friends(lay):
    return [
        lay.moved(**{"d" + axis: d, "dc": c})
        for axis in "xyz" for d in range(4) for c in range(lay.cores) if (d, c) != (0, 0)
    ]


def kernel(lay, count_x, count_y, cap, sizes, *refs):
    places, patches, *inputs = refs[:9]
    solution, residual, sums = refs[9:12]
    solve_refs = refs[12 : 12 + sizes[0]]
    exchange_refs = refs[12 + sizes[0] : 12 + sizes[0] + sizes[1]]
    surface, load_sem = refs[12 + sizes[0] + sizes[1] :]
    solve = Solve(lay, count_x, count_y, solve_refs)
    held = exchange_refs[0]
    load = pltpu.make_async_copy(patches, held, load_sem.at[0])
    load.start()
    loads = [
        pltpu.make_async_copy(source, target, load_sem.at[i + 1])
        for i, (source, target) in enumerate(zip(inputs, solve_refs[:7]))
    ]
    for i in (1, 6, 2, 3, 4, 5, 0):
        loads[i].start()
    solve.loads = loads
    friends = exchange_friends(lay) + solve_friends(lay, count_x, count_y)
    barrier = pltpu.get_barrier_semaphore()
    for friend in friends:
        pl.semaphore_signal(barrier, inc=1, device_id=friend, device_id_type=MESH)
    early = exchange_body(
        lay, cap, solve, lambda: pl.semaphore_wait(barrier, len(friends)), load, places, surface,
        *exchange_refs,
    )
    solve.start(0, 1, surface)
    late = solve.send(0, 0, 1, False)
    for copy in early:
        copy.wait()
    solve.apply(2, 4, solve.layers)
    for j in range(3):
        for copy in late:
            copy.wait()
        solve.apply(j, 0, j + 2)
        if j < 2:
            late = solve.send(j + 1, 0, j + 2, False)
    weight_v = exchange_refs[8]
    total = solve.total(weight_v[6:7, :])
    sums[...] = total
    solve.finish(total, solution, residual)


def run(lay, count_x, count_y, cap, places, patches, *grids):
    layers, rows, cols = grids[0].shape
    solve = solve_scratch(lay, layers, rows, cols)
    moving = exchange_scratch(cap, patches.shape[1])
    return pl.pallas_call(
        functools.partial(kernel, lay, count_x, count_y, cap, (len(solve), len(moving))),
        out_shape=[jax.ShapeDtypeStruct((layers, rows, cols), jnp.float32)] * 2
        + [jax.ShapeDtypeStruct((8, 128), jnp.float32)],
        in_specs=[pl.BlockSpec(memory_space=pltpu.VMEM)]
        + [pl.BlockSpec(memory_space=pl.ANY)] * (1 + len(grids)),
        out_specs=[pl.BlockSpec(memory_space=pltpu.VMEM)] * 3,
        scratch_shapes=solve + moving + [
            pltpu.VMEM((rows, cols), jnp.float32), pltpu.SemaphoreType.DMA((8,))
        ],
        compiler_params=pltpu.CompilerParams(
            collective_id=cap, has_side_effects=True,
            vmem_limit_bytes=(42 if cap == 1 else 60) * MIB,
        ),
    )(places, patches, *grids)


def on_device(forcing, patches, owners, slots, cond_x, cond_y, cond_z, storage, fixed, closed):
    count_x, count_y = lax.axis_size("gx"), lax.axis_size("gy")
    lay = Layout(count_x, count_y)
    places = owners * 2 + slots
    args = (places, patches, forcing, cond_x, cond_y, cond_z, storage, fixed, closed)
    *quick, sums = run(lay, count_x, count_y, 1, *args)

    def general(args, quick):
        return tuple(run(lay, count_x, count_y, 2, *args)[:2])

    return lax.cond(sums[6, 0] > 0.0, general, lambda args, quick: quick, args, tuple(quick))


def solution(mesh):
    grid = P(None, "gx", "gy")
    return jax.shard_map(
        on_device,
        mesh=mesh,
        in_specs=(grid, P("gx", "gy", None), P("gx", "gy"), P("gx", "gy")) + (grid,) * 6,
        out_specs=(grid, grid),
        check_vma=False,
    )
```

time: 120 us -> 85.8 us (0.71); the launches traced: 118 us -> 85.3 us
  Pallas kernels: 112 us -> 77.4 us
    pallas_call x2 -> x1, Pallas kernels: 112 us -> 77.4 us  [run(): pl.pallas_call(functools.partial(kernel, lay, count_x, count_y, cap, (len...]
    unnamed x12 -> x9, local copies, waits for them, and re-layouts: 5.66 us -> 5.32 us
where the time goes in v3:
time: 85.8 us; the launch traced here: 85.3 us
  Pallas kernels  77.4 us (90%)
  local copies, waits for them, and re-layouts  5.95 us (7%)
  between operations  1.35 us (2%)
    pallas_call x1, Pallas kernels, run(): pl.pallas_call(functools.partial(kernel, lay, count_x, count_y, cap, (len...  77.4 us
    unnamed x9, local copies, waits for them, and re-layouts  5.32 us

profile of v3, /device:TPU:1, one launch (start us, length us, event | category | flops | bytes accessed | tf_op | source)
XLA Modules:
  0.0 85.3 jit_solution(10833234742151945125)
XLA Ops:
  0.6 0.7 broadcast_multiply_fusion
  1.3 0.1 copy.19
  1.4 0.8 copy.20
  2.2 0.0 copy-start
  2.2 0.0 copy-start.1
  2.2 0.0 copy-start.2
  2.2 77.4 %shard_map.117 = (f32[8,128,256]{2,1,0:T(8,128)}, f32[8,128,256]{2,1,0:T(8,128)}, f32[8,128]{1,0:T(8,128)S(1)}) custom-call(s32[128,1]{1,0:T(8,128)S(1)} %add.3.refs_0_, bf16[128,128,128]{2,1,0:T(8,128)(2,1)} %refs_1_.1, f32[8,128,256]{2,1,0:T(8,128)} %refs_2_.1, f32[8,128,256]{2,1,0:T(8,128)} %refs_3_.1, f32[8,128,256]{2,1,0:T(8,128)} %refs_4_.1, ...), custom_call_target="tpu_custom_call" | custom-call | tf_op jit(solution)/shard_map/pallas_call | solution.py:728
  79.6 0.5 slice.3
  80.8 0.0 copy-done
  80.8 0.0 copy-done.1
  80.8 0.0 copy-done.2
  80.8 2.3 %copy.27 = f32[8,128,256]{2,1,0:T(8,128)} copy(f32[8,128,256]{2,1,0:T(8,128)} %get-tuple-element.51) | data formatting | bytes 2097152
  83.1 2.3 %copy.28 = f32[8,128,256]{2,1,0:T(8,128)} copy(f32[8,128,256]{2,1,0:T(8,128)} %get-tuple-element.52) | data formatting | bytes 2097152
  (2 shorter events, 0.0 us)
Async XLA Ops:
  2.2 78.6 %copy-start = (f32[8,128,256]{2,1,0:T(8,128)S(1)}, f32[8,128,256]{2,1,0:T(8,128)}, u32[]{:S(2)}) copy-start(f32[8,128,256]{2,1,0:T(8,128)} %refs_2_.1) | copy-start | bytes 3145732
  2.2 78.6 %copy-start.1 = (f32[8,128,256]{2,1,0:T(8,128)S(1)}, f32[8,128,256]{2,1,0:T(8,128)}, u32[]{:S(2)}) copy-start(f32[8,128,256]{2,1,0:T(8,128)} %refs_3_.1) | copy-start | bytes 3145732
  2.2 78.6 %copy-start.2 = (f32[8,128,256]{2,1,0:T(8,128)S(1)}, f32[8,128,256]{2,1,0:T(8,128)}, u32[]{:S(2)}) copy-start(f32[8,128,256]{2,1,0:T(8,128)} %refs_4_.1) | copy-start | bytes 3145732

commit v4 on v3

--- a/solution.py
+++ b/solution.py
@@ -79,6 +79,10 @@
         )
         self.zero = jnp.zeros((8, self.cols), jnp.float32)
         self.moments = [self.zero] * 6
+
+    def start_loads(self):
+        for i in (1, 6, 2, 3, 4, 5, 0):
+            self.loads[i].start()
 
     def load_faces(self):
         for i in (1, 6, 2, 3):
@@ -318,13 +322,14 @@
     ]
 
 
-def solve_friends(lay, count_x, count_y):
+def every_friend(lay, count_x):
     gx, gy = lax.axis_index("gx"), lax.axis_index("gy")
-    friends = [((gx + 1) % count_x, gy), ((gx + count_x - 1) % count_x, gy),
-               (gx, (gy + 1) % count_y), (gx, (gy + count_y - 1) % count_y)]
-    for peers in lay.stages():
-        friends += [lay.moved(**offset) for offset in peers]
-    return friends
+    friends = [((gx + 1) % count_x, gy), ((gx + count_x - 1) % count_x, gy), lay.moved(dc=1)]
+    for axis in "xyz":
+        friends += [
+            lay.moved(**{"d" + axis: d, "dc": c}) for d in range(1, 4) for c in range(lay.cores)
+        ]
+    return friends + [lay.moved(dx=x, dz=z) for x in range(1, 4) for z in range(1, 4)]
 
 
 def scalars(total):
@@ -386,7 +391,7 @@
 
 
 def exchange_body(
-    lay, cap, solve, enter, load, places, surface, held, packed, arrived, summed, landed, second,
+    lay, cap, solve, enter, load, owners, slots, surface, held, packed, arrived, summed, landed, second,
     third, index_v, weight_v, weight_in, index_s, weight_s, move_sem,
     send1, recv1, send1w, recv1w, send2, recv2, send3, recv3, *star,
 ):
@@ -397,8 +402,14 @@
 
     shape = (per_device, 128)
     patch_ids = lax.broadcasted_iota(jnp.int32, shape, 0)
-    place = jnp.broadcast_to(places[...], shape) - 2 * lax.broadcasted_iota(jnp.int32, shape, 1)
-    hit = jnp.logical_or(place == 0, place == 1)
+    row = (owners[...] * 2 + slots[...]).astype(jnp.float32)
+    column = jnp.sum(
+        jnp.where(solve.eye, jnp.broadcast_to(row, shape), 0.0), axis=1, keepdims=True
+    )
+    place = jnp.broadcast_to(column, shape) - (
+        2 * lax.broadcasted_iota(jnp.int32, shape, 1)
+    ).astype(jnp.float32)
+    hit = jnp.logical_or(place == 0.0, place == 1.0)
     first = jnp.min(jnp.where(hit, patch_ids, per_device), axis=0, keepdims=True)
     last = jnp.max(jnp.where(hit, patch_ids, -1), axis=0, keepdims=True)
     index_v[0:1, :] = jnp.minimum(first, per_device - 1)
@@ -411,7 +422,7 @@
         chosen = jnp.logical_and(hit, chosen)
         for s in range(2):
             weight_v[2 * j + s : 2 * j + s + 1, :] = jnp.sum(
-                jnp.where(jnp.logical_and(chosen, place == s), 1.0, 0.0), axis=0, keepdims=True
+                jnp.where(jnp.logical_and(chosen, place == float(s)), 1.0, 0.0), axis=0, keepdims=True
             )
     doubled = jnp.where(again, 1.0, 0.0)
     for s in range(2):
@@ -433,9 +444,17 @@
     def moved(axis, d, c):
         return lay.moved(**{"d" + axis: d, "dc": c})
 
-    solve.load_faces()
-    solve.faces()
-    load.wait()
+    weight_copies = [
+        [
+            remote(weight_v, weight_in.at[q, i], send1w.at[q, i], recv1w.at[q, i],
+                   moved(order[0], d, c))
+            for i, (d, c) in enumerate(offsets)
+        ]
+        for q, order in enumerate(ORDERS)
+    ]
+    for copy in load:
+        copy.wait()
+    solve.start_loads()
     to_scalar.wait()
     own_weight.wait()
 
@@ -449,65 +468,44 @@
     if common:
         common.pack(index_s[2, 0])
     enter()
-    solve.send_rims()
+    for group in weight_copies:
+        for copy in group:
+            copy.start()
     if common:
         common.scatter()
-    weight_copies = []
-    for q, order in enumerate(ORDERS):
-        weight_copies.append([
-            remote(weight_v, weight_in.at[q, i], send1w.at[q, i], recv1w.at[q, i],
-                   moved(order[0], d, c))
-            for i, (d, c) in enumerate(offsets)
-        ])
-        for copy in weight_copies[-1]:
-            copy.start()
-
-
-    def outgoing(q, a, c):
-        at = pl.ds(*parts[q])
-        axis = ORDERS[q][0]
-        if axis == "x":
-            return packed.at[a, :, c, :, :, at, :]
-        if axis == "y":
-            return packed.at[:, :, c, a, :, at, :]
-        return packed.at[:, a, c, :, :, at, :]
-
-    copies1 = []
-    for i, (d, c) in enumerate(offsets):
-        for q, order in enumerate(ORDERS):
-            axis = order[0]
-            copy = remote(
-                outgoing(q, (me[axis] + d) % 4, (me["c"] + c) % lay.cores),
-                arrived[q].at[i], send1.at[q, i], recv1.at[q, i], moved(axis, d, c),
-            )
-            copy.start()
-            copies1.append((q, copy))
-
-    solve.load_rest()
-    solve.prepare()
-    solve.start(1, solve.layers)
-    early = solve.send(0, 1, solve.layers, True)
-    for copy in weight_copies[1]:
-        copy.wait()
-    if common:
-        common.reduce()
-    copies2, copies3 = [], []
-    for q, order in enumerate(ORDERS):
-        for copy in weight_copies[q]:
-            if q != 1:
-                copy.wait()
-        gather = pltpu.make_async_copy(weight_in.at[q], weight_s.at[q, pl.ds(1, 7)], move_sem.at[2 + q])
-        gather.start()
-        gather.wait()
-        for p, copy in copies1:
-            if p == q:
-                copy.wait()
+
+    def first_stage(half):
+        some = pl.ds(2 * half, 2)
+        copies = [[], [], []]
+        for i, (d, c) in enumerate(offsets):
+            for q, order in enumerate(ORDERS):
+                axis = order[0]
+                at = pl.ds(*parts[q])
+                a, core = (me[axis] + d) % 4, (me["c"] + c) % lay.cores
+                if axis == "x":
+                    source = packed.at[a, some, core, :, :, at, :]
+                elif axis == "y":
+                    source = packed.at[some, :, core, a, :, at, :]
+                else:
+                    source = packed.at[:, a, core, some, :, at, :]
+                target = arrived[q].at[i, :, some] if axis == "z" else arrived[q].at[i, some]
+                copy = remote(source, target, send1.at[half, q, i], recv1.at[half, q, i],
+                              moved(axis, d, c))
+                copy.start()
+                copies[q].append(copy)
+        return copies
+
+    def second_stage(half, q, copies):
+        order = ORDERS[q]
+        for copy in copies[q]:
+            copy.wait()
         at = pl.ds(*parts[q])
         rows = parts[q][1]
         dims = DIMS[order[0]]
 
-        def reduce(k, carry, q=q, order=order, at=at, rows=rows, dims=dims):
-            spot = {dims[0]: k // 4, dims[1]: k % 4, order[0]: me[order[0]]}
+        def reduce(k, carry):
+            b, c = k // 2, 2 * half + k % 2
+            spot = {order[0]: me[order[0]], order[1]: b, order[2]: c}
             owner = spot["x"] * 32 + spot["z"] * 8 + me["c"] * 4 + spot["y"]
             sums = [jnp.zeros((rows, side), jnp.float32) for _ in range(2)]
             for source in range(8):
@@ -515,32 +513,60 @@
                     if source == 0:
                         value = packed[spot["x"], spot["z"], me["c"], spot["y"], j, at, :]
                     else:
-                        value = arrived[q][source - 1, k // 4, k % 4, j]
+                        value = arrived[q][source - 1, spot[dims[0]], spot[dims[1]], j]
                     value = value.astype(jnp.float32)
                     table = (0, 0) if source == 0 else (q, source)
                     for s in range(2):
                         sums[s] = sums[s] + weight_s[(*table, 2 * j + s, owner)] * value
             for s in range(2):
-                summed[q][spot[order[1]], spot[order[2]], s] = sums[s]
+                summed[q][b, c, s] = sums[s]
             return carry
 
-        lax.fori_loop(0, 16, reduce, 0)
+        lax.fori_loop(0, 8, reduce, 0)
+        some = pl.ds(2 * half, 2)
         mine = []
         for d in range(1, 4):
-            copy = remote(summed[q].at[(me[order[1]] + d) % 4], landed[q].at[d - 1],
-                          send2.at[q, d - 1], recv2.at[q, d - 1], moved(order[1], d, 0))
+            copy = remote(summed[q].at[(me[order[1]] + d) % 4, some], landed[q].at[d - 1, some],
+                          send2.at[half, q, d - 1], recv2.at[half, q, d - 1],
+                          moved(order[1], d, 0))
             copy.start()
             mine.append(copy)
-        copies2.append(mine)
+        return mine
+
+    copies1 = [first_stage(0)]
+    solve.load_faces()
+    solve.faces()
+    solve.send_rims()
+    copies1.append(first_stage(1))
+    gathers = []
+    for q in range(3):
+        for copy in weight_copies[q]:
+            copy.wait()
+        gathers.append(pltpu.make_async_copy(
+            weight_in.at[q], weight_s.at[q, pl.ds(1, 7)], move_sem.at[2 + q]
+        ))
+        gathers[q].start()
+    for gather in gathers:
+        gather.wait()
+    copies2 = [[second_stage(0, q, copies1[0]) for q in range(3)]]
+    solve.load_rest()
+    solve.prepare()
+    solve.start(1, solve.layers)
+    early = solve.send(0, 1, solve.layers, True)
+    if common:
+        common.reduce()
+    copies2.append([second_stage(1, q, copies1[1]) for q in range(3)])
     for copy in early:
         copy.wait()
     solve.apply(0, 2, solve.layers)
     early = solve.send(1, 2, solve.layers, True)
     if common:
         common.gather()
+    copies3 = []
     for q, order in enumerate(ORDERS):
-        for copy in copies2[q]:
-            copy.wait()
+        for half in range(2):
+            for copy in copies2[half][q]:
+                copy.wait()
 
         def reduce(k, carry, q=q, order=order):
             total = summed[q][me[order[1]], k]
@@ -662,8 +688,8 @@
         pltpu.VMEM((3, 7, 8, 128), jnp.float32),
         pltpu.SMEM((8, 128), jnp.int32), pltpu.SMEM((3, 8, 8, 128), jnp.float32),
         dma((5,)),
-        dma((3, 7)), dma((3, 7)), dma((3, 7)), dma((3, 7)),
-        dma((3, 3)), dma((3, 3)), dma((3, 3)), dma((3, 3)),
+        dma((2, 3, 7)), dma((2, 3, 7)), dma((3, 7)), dma((3, 7)),
+        dma((2, 3, 3)), dma((2, 3, 3)), dma((3, 3)), dma((3, 3)),
     ] + ([
         pltpu.VMEM((8, 16, side), bf16), pltpu.VMEM((7, 16, side), bf16),
         pltpu.VMEM((2, 2, 16, side), jnp.float32), pltpu.VMEM((15, 2, 16, side), jnp.float32),
@@ -672,36 +698,34 @@
     ] if cap == 1 else [])
 
 
-def exchange_friends(lay):
-    return [
-        lay.moved(**{"d" + axis: d, "dc": c})
-        for axis in "xyz" for d in range(4) for c in range(lay.cores) if (d, c) != (0, 0)
-    ]
-
-
 def kernel(lay, count_x, count_y, cap, sizes, *refs):
-    places, patches, *inputs = refs[:9]
-    solution, residual, sums = refs[9:12]
-    solve_refs = refs[12 : 12 + sizes[0]]
-    exchange_refs = refs[12 + sizes[0] : 12 + sizes[0] + sizes[1]]
-    surface, load_sem = refs[12 + sizes[0] + sizes[1] :]
+    owners, slots, patches, *inputs = refs[:10]
+    solution, residual, sums = refs[10:13]
+    solve_refs = refs[13 : 13 + sizes[0]]
+    exchange_refs = refs[13 + sizes[0] : 13 + sizes[0] + sizes[1]]
+    surface, load_sem = refs[13 + sizes[0] + sizes[1] :]
     solve = Solve(lay, count_x, count_y, solve_refs)
     held = exchange_refs[0]
-    load = pltpu.make_async_copy(patches, held, load_sem.at[0])
-    load.start()
+    some = held.shape[0] // 4
+    load = [
+        pltpu.make_async_copy(
+            patches.at[pl.ds(i * some, some)], held.at[pl.ds(i * some, some)], load_sem.at[7 + i]
+        )
+        for i in range(4)
+    ]
+    for copy in load:
+        copy.start()
     loads = [
-        pltpu.make_async_copy(source, target, load_sem.at[i + 1])
+        pltpu.make_async_copy(source, target, load_sem.at[i])
         for i, (source, target) in enumerate(zip(inputs, solve_refs[:7]))
     ]
-    for i in (1, 6, 2, 3, 4, 5, 0):
-        loads[i].start()
     solve.loads = loads
-    friends = exchange_friends(lay) + solve_friends(lay, count_x, count_y)
+    friends = every_friend(lay, count_x)
     barrier = pltpu.get_barrier_semaphore()
     for friend in friends:
         pl.semaphore_signal(barrier, inc=1, device_id=friend, device_id_type=MESH)
     early = exchange_body(
-        lay, cap, solve, lambda: pl.semaphore_wait(barrier, len(friends)), load, places, surface,
+        lay, cap, solve, lambda: pl.semaphore_wait(barrier, len(friends)), load, owners, slots, surface,
         *exchange_refs,
     )
     solve.start(0, 1, surface)
@@ -721,7 +745,24 @@
     solve.finish(total, solution, residual)
 
 
-def run(lay, count_x, count_y, cap, places, patches, *grids):
+def move_kernel(a, b, c, d):
+    c[...] = a[...]
+    d[...] = b[...]
+
+
+def move(*arrays):
+    layers, rows, cols = arrays[0].shape
+    block = pl.BlockSpec((layers // 4, rows, cols), lambda i: (i, 0, 0))
+    return tuple(pl.pallas_call(
+        move_kernel,
+        grid=(4,),
+        out_shape=[jax.ShapeDtypeStruct(x.shape, x.dtype) for x in arrays],
+        in_specs=[block] * 2,
+        out_specs=[block] * 2,
+    )(*arrays))
+
+
+def run(lay, count_x, count_y, cap, owners, slots, patches, *grids):
     layers, rows, cols = grids[0].shape
     solve = solve_scratch(lay, layers, rows, cols)
     moving = exchange_scratch(cap, patches.shape[1])
@@ -729,30 +770,29 @@
         functools.partial(kernel, lay, count_x, count_y, cap, (len(solve), len(moving))),
         out_shape=[jax.ShapeDtypeStruct((layers, rows, cols), jnp.float32)] * 2
         + [jax.ShapeDtypeStruct((8, 128), jnp.float32)],
-        in_specs=[pl.BlockSpec(memory_space=pltpu.VMEM)]
+        in_specs=[pl.BlockSpec(memory_space=pltpu.VMEM)] * 2
         + [pl.BlockSpec(memory_space=pl.ANY)] * (1 + len(grids)),
         out_specs=[pl.BlockSpec(memory_space=pltpu.VMEM)] * 3,
         scratch_shapes=solve + moving + [
-            pltpu.VMEM((rows, cols), jnp.float32), pltpu.SemaphoreType.DMA((8,))
+            pltpu.VMEM((rows, cols), jnp.float32), pltpu.SemaphoreType.DMA((11,))
         ],
         compiler_params=pltpu.CompilerParams(
             collective_id=cap, has_side_effects=True,
             vmem_limit_bytes=(42 if cap == 1 else 60) * MIB,
         ),
-    )(places, patches, *grids)
+    )(owners, slots, patches, *grids)
 
 
 def on_device(forcing, patches, owners, slots, cond_x, cond_y, cond_z, storage, fixed, closed):
     count_x, count_y = lax.axis_size("gx"), lax.axis_size("gy")
     lay = Layout(count_x, count_y)
-    places = owners * 2 + slots
-    args = (places, patches, forcing, cond_x, cond_y, cond_z, storage, fixed, closed)
+    args = (owners.T, slots.T, patches, forcing, cond_x, cond_y, cond_z, storage, fixed, closed)
     *quick, sums = run(lay, count_x, count_y, 1, *args)
 
     def general(args, quick):
         return tuple(run(lay, count_x, count_y, 2, *args)[:2])
 
-    return lax.cond(sums[6, 0] > 0.0, general, lambda args, quick: quick, args, tuple(quick))
+    return move(*lax.cond(sums[6, 0] > 0.0, general, lambda args, quick: quick, args, tuple(quick)))
 
 
 def solution(mesh):

time: 85.8 us -> 79 us (0.921)
  local copies, waits for them, and re-layouts: 5.95 us -> 0.53 us
    unnamed x9 -> x10, local copies, waits for them, and re-layouts: 5.32 us -> 0.02 us
    pallas_call x1, Pallas kernels: 77.4 us -> 73.2 us  [run(): pl.pallas_call(functools.partial(kernel, lay, count_x, count_y, cap, (len...]
    pallas_call x0 -> x1, Pallas kernels: none -> 3.75 us  [move(): pl.pallas_call(move_kernel, grid=(4,), out_shape=[jax.ShapeDtypeStruct(x....]
where the time goes in v4:
time: 79 us; the launch traced here: 78.9 us
  Pallas kernels  76.9 us (97%)
  between operations  1.38 us (2%)
    pallas_call x1, Pallas kernels, run(): pl.pallas_call(functools.partial(kernel, lay, count_x, count_y, cap, (len...  73.2 us
    pallas_call x1, Pallas kernels, move(): pl.pallas_call(move_kernel, grid=(4,), out_shape=[jax.ShapeDtypeStruct(x....  3.75 us

profile of v4, /device:TPU:1, one launch (start us, length us, event | category | flops | bytes accessed | tf_op | source)
XLA Modules:
  0.0 78.9 jit_solution(5340933261409284021)
XLA Ops:
  0.6 0.0 copy-start
  0.6 0.0 copy-start.1
  0.7 0.0 copy-start.2
  0.7 0.0 copy-start.3
  0.7 0.0 copy-start.4
  0.7 73.2 %shard_map.113 = (f32[8,128,256]{2,1,0:T(8,128)}, f32[8,128,256]{2,1,0:T(8,128)}, f32[8,128]{1,0:T(8,128)S(1)}) custom-call(s32[1,128]{1,0:T(1,128)} %bitcast.3, s32[1,128]{1,0:T(1,128)} %bitcast.5, bf16[128,128,128]{2,1,0:T(8,128)(2,1)} %refs_2_.1, f32[8,128,256]{2,1,0:T(8,128)} %refs_3_.1, f32[8,128,256]{2,1,0:T(8,128)} %refs_4_.1, ...), custom_call_target="tpu_custom_call" | custom-call | tf_op jit(solution)/shard_map/pallas_call | solution.py:769
  73.9 0.5 slice.3
  75.0 0.0 copy-done
  75.0 0.0 copy-done.1
  75.1 0.0 copy-done.2
  75.1 0.0 copy-done.3
  75.1 0.0 copy-done.4
  75.1 3.8 %shard_map.114 = (f32[8,128,256]{2,1,0:T(8,128)}, f32[8,128,256]{2,1,0:T(8,128)}) custom-call(f32[8,128,256]{2,1,0:T(8,128)} %get-tuple-element.46.a, f32[8,128,256]{2,1,0:T(8,128)} %get-tuple-element.47.b), custom_call_target="tpu_custom_call" | custom-call | tf_op jit(solution)/shard_map/pallas_call | solution.py:756
  (1 shorter events, 0.0 us)
Async XLA Ops:
  0.6 74.4 %copy-start = (f32[8,128,256]{2,1,0:T(8,128)S(1)}, f32[8,128,256]{2,1,0:T(8,128)}, u32[]{:S(2)}) copy-start(f32[8,128,256]{2,1,0:T(8,128)} %refs_3_.1) | copy-start | bytes 3145732
  0.6 74.4 %copy-start.1 = (f32[8,128,256]{2,1,0:T(8,128)S(1)}, f32[8,128,256]{2,1,0:T(8,128)}, u32[]{:S(2)}) copy-start(f32[8,128,256]{2,1,0:T(8,128)} %refs_4_.1) | copy-start | bytes 3145732
  0.7 74.4 %copy-start.2 = (f32[8,128,256]{2,1,0:T(8,128)S(1)}, f32[8,128,256]{2,1,0:T(8,128)}, u32[]{:S(2)}) copy-start(f32[8,128,256]{2,1,0:T(8,128)} %refs_5_.1) | copy-start | bytes 3145732
  0.7 74.4 %copy-start.3 = (s32[128,1]{0,1:T(1,128)S(1)}, s32[128,1]{0,1:T(1,128)}, u32[]{:S(2)}) copy-start(s32[128,1]{0,1:T(1,128)} %param.14) | copy-start | bytes 1540
  0.7 74.4 %copy-start.4 = (s32[128,1]{0,1:T(1,128)S(1)}, s32[128,1]{0,1:T(1,128)}, u32[]{:S(2)}) copy-start(s32[128,1]{0,1:T(1,128)} %param.15) | copy-start | bytes 1540

commit v5 on v4

--- a/solution.py
+++ b/solution.py
@@ -191,13 +191,6 @@
     def send(self, j, low, high, early):
         rows, cols = self.rows, self.cols
 
-        def body(layer, carry):
-            here = self.tees.at[j, layer, pl.ds(PAD, rows), :]
-            self.col_out[j + 1, 0, pl.ds(layer, 1), :] = self.column(here[:, cols - 1 : cols])
-            self.col_out[j + 1, 1, pl.ds(layer, 1), :] = self.column(here[:, 0:1])
-            return carry
-
-        lax.fori_loop(low, high, body, 0)
         some = pl.ds(low, high - low)
         tee = self.tees.at[j, some]
         k = 2 * j + 1 + early
@@ -211,7 +204,17 @@
             remote(self.col_out.at[j + 1, 1, some], self.col_in.at[j + 1, 1, some],
                    self.halo_send.at[k, 3], self.halo_recv.at[k, 3], self.down),
         ]
-        for copy in copies:
+        for copy in copies[:2]:
+            copy.start()
+
+        def body(layer, carry):
+            here = self.tees.at[j, layer, pl.ds(PAD, rows), :]
+            self.col_out[j + 1, 0, pl.ds(layer, 1), :] = self.column(here[:, cols - 1 : cols])
+            self.col_out[j + 1, 1, pl.ds(layer, 1), :] = self.column(here[:, 0:1])
+            return carry
+
+        lax.fori_loop(low, high, body, 0)
+        for copy in copies[2:]:
             copy.start()
         return copies
 
@@ -280,7 +283,13 @@
             partial[s + 1] = total
         return partial[len(self.lay.stages())]
 
-    def finish(self, total, solution, residual):
+    def finish(self, total, solution, residual, outs, sem):
+        def leave(layer):
+            return [
+                pltpu.make_async_copy(source.at[layer], target.at[layer], sem.at[k, layer])
+                for k, (source, target) in enumerate(zip((solution, residual), outs))
+            ]
+
         sol_w, res_w = scalars(total)
         step = self.step
 
@@ -297,9 +306,14 @@
                 for j in range(1, 4):
                     out += res_w[j] * self.enns[j, layer, at, :]
                 residual[layer, at, :] = keep * out
+            for copy in leave(layer):
+                copy.start()
             return carry
 
         lax.fori_loop(0, self.layers, body, 0)
+        for layer in range(self.layers):
+            for copy in leave(layer):
+                copy.wait()
 
 
 def solve_scratch(lay, layers, rows, cols):
@@ -385,9 +399,9 @@
 
 
 def portions(side):
-    tiles = side // 16
-    cut = [0, -(-tiles // 3), -(-2 * tiles // 3), tiles]
-    return [(16 * cut[i], 16 * (cut[i + 1] - cut[i])) for i in range(3)]
+    tiles = side // 8
+    cut = [0, tiles // 3, tiles - tiles // 3, tiles]
+    return [(8 * cut[i], 8 * (cut[i + 1] - cut[i])) for i in range(3)]
 
 
 def exchange_body(
@@ -700,10 +714,10 @@
 
 def kernel(lay, count_x, count_y, cap, sizes, *refs):
     owners, slots, patches, *inputs = refs[:10]
-    solution, residual, sums = refs[10:13]
+    *outs, sums = refs[10:13]
     solve_refs = refs[13 : 13 + sizes[0]]
     exchange_refs = refs[13 + sizes[0] : 13 + sizes[0] + sizes[1]]
-    surface, load_sem = refs[13 + sizes[0] + sizes[1] :]
+    surface, load_sem, solution, residual, leave_sem = refs[13 + sizes[0] + sizes[1] :]
     solve = Solve(lay, count_x, count_y, solve_refs)
     held = exchange_refs[0]
     some = held.shape[0] // 4
@@ -734,31 +748,43 @@
         copy.wait()
     solve.apply(2, 4, solve.layers)
     for j in range(3):
+        solve.apply(j, j + 1, j + 2)
         for copy in late:
             copy.wait()
-        solve.apply(j, 0, j + 2)
+        solve.apply(j, 0, j + 1)
         if j < 2:
             late = solve.send(j + 1, 0, j + 2, False)
     weight_v = exchange_refs[8]
     total = solve.total(weight_v[6:7, :])
     sums[...] = total
-    solve.finish(total, solution, residual)
-
-
-def move_kernel(a, b, c, d):
-    c[...] = a[...]
-    d[...] = b[...]
+    solve.finish(total, solution, residual, outs, leave_sem)
+
+
+def move_kernel(a, b, c, d, held, sem):
+    layers = a.shape[0]
+    into = [pltpu.make_async_copy(x.at[i], held.at[k, i], sem.at[0, k, i])
+            for i in range(layers) for k, x in enumerate((a, b))]
+    away = [pltpu.make_async_copy(held.at[k, i], x.at[i], sem.at[1, k, i])
+            for i in range(layers) for k, x in enumerate((c, d))]
+    for copy in into:
+        copy.start()
+    for first, then in zip(into, away):
+        first.wait()
+        then.start()
+    for copy in away:
+        copy.wait()
 
 
 def move(*arrays):
-    layers, rows, cols = arrays[0].shape
-    block = pl.BlockSpec((layers // 4, rows, cols), lambda i: (i, 0, 0))
+    shape = arrays[0].shape
     return tuple(pl.pallas_call(
         move_kernel,
-        grid=(4,),
         out_shape=[jax.ShapeDtypeStruct(x.shape, x.dtype) for x in arrays],
-        in_specs=[block] * 2,
-        out_specs=[block] * 2,
+        in_specs=[pl.BlockSpec(memory_space=pl.ANY)] * 2,
+        out_specs=[pl.BlockSpec(memory_space=pl.ANY)] * 2,
+        scratch_shapes=[
+            pltpu.VMEM((2, *shape), jnp.float32), pltpu.SemaphoreType.DMA((2, 2, shape[0]))
+        ],
     )(*arrays))
 
 
@@ -772,9 +798,13 @@
         + [jax.ShapeDtypeStruct((8, 128), jnp.float32)],
         in_specs=[pl.BlockSpec(memory_space=pltpu.VMEM)] * 2
         + [pl.BlockSpec(memory_space=pl.ANY)] * (1 + len(grids)),
-        out_specs=[pl.BlockSpec(memory_space=pltpu.VMEM)] * 3,
+        out_specs=[pl.BlockSpec(memory_space=pl.ANY)] * 2
+        + [pl.BlockSpec(memory_space=pltpu.VMEM)],
         scratch_shapes=solve + moving + [
-            pltpu.VMEM((rows, cols), jnp.float32), pltpu.SemaphoreType.DMA((11,))
+            pltpu.VMEM((rows, cols), jnp.float32), pltpu.SemaphoreType.DMA((11,)),
+            pltpu.VMEM((layers, rows, cols), jnp.float32),
+            pltpu.VMEM((layers, rows, cols), jnp.float32),
+            pltpu.SemaphoreType.DMA((2, layers)),
         ],
         compiler_params=pltpu.CompilerParams(
             collective_id=cap, has_side_effects=True,

time: 79 us -> 75.1 us (0.951)
  Pallas kernels: 76.9 us -> 73.1 us
    pallas_call x1, Pallas kernels: 73.2 us -> 70.5 us  [run(): pl.pallas_call(functools.partial(kernel, lay, count_x, count_y, cap, (len...]
    pallas_call x1, Pallas kernels: 3.75 us -> 2.57 us  [move(): pl.pallas_call(move_kernel, out_shape=[jax.ShapeDtypeStruct(x.shape, x.dt...]
where the time goes in v5:
time: 75.1 us; the launch traced here: 75 us
  Pallas kernels  73.1 us (97%)
  between operations  1.38 us (2%)
    pallas_call x1, Pallas kernels, run(): pl.pallas_call(functools.partial(kernel, lay, count_x, count_y, cap, (len...  70.5 us
    pallas_call x1, Pallas kernels, move(): pl.pallas_call(move_kernel, out_shape=[jax.ShapeDtypeStruct(x.shape, x.dt...  2.57 us

profile of v5, /device:TPU:1, one launch (start us, length us, event | category | flops | bytes accessed | tf_op | source)
XLA Modules:
  0.0 75.0 jit_solution(215625705755911444)
XLA Ops:
  0.6 0.0 copy-start
  0.6 0.0 copy-start.1
  0.7 0.0 copy-start.2
  0.7 0.0 copy-start.3
  0.7 0.0 copy-start.4
  0.7 70.5 %shard_map.113 = (f32[8,128,256]{2,1,0:T(8,128)}, f32[8,128,256]{2,1,0:T(8,128)}, f32[8,128]{1,0:T(8,128)S(1)}) custom-call(s32[1,128]{1,0:T(1,128)} %bitcast.3, s32[1,128]{1,0:T(1,128)} %bitcast.5, bf16[128,128,128]{2,1,0:T(8,128)(2,1)} %refs_2_.1, f32[8,128,256]{2,1,0:T(8,128)} %refs_3_.1, f32[8,128,256]{2,1,0:T(8,128)} %refs_4_.1, ...), custom_call_target="tpu_custom_call" | custom-call | tf_op jit(solution)/shard_map/pallas_call | solution.py:795
  71.2 0.5 slice.3
  72.3 0.0 copy-done
  72.4 0.0 copy-done.1
  72.4 0.0 copy-done.2
  72.4 0.0 copy-done.3
  72.4 0.0 copy-done.4
  72.4 2.6 %shard_map.114 = (f32[8,128,256]{2,1,0:T(8,128)}, f32[8,128,256]{2,1,0:T(8,128)}) custom-call(f32[8,128,256]{2,1,0:T(8,128)} %get-tuple-element.46.a, f32[8,128,256]{2,1,0:T(8,128)} %get-tuple-element.47.b), custom_call_target="tpu_custom_call" | custom-call | tf_op jit(solution)/shard_map/pallas_call | solution.py:780
  (1 shorter events, 0.0 us)
Async XLA Ops:
  0.6 71.7 %copy-start = (f32[8,128,256]{2,1,0:T(8,128)S(1)}, f32[8,128,256]{2,1,0:T(8,128)}, u32[]{:S(2)}) copy-start(f32[8,128,256]{2,1,0:T(8,128)} %refs_3_.1) | copy-start | bytes 3145732
  0.6 71.7 %copy-start.1 = (f32[8,128,256]{2,1,0:T(8,128)S(1)}, f32[8,128,256]{2,1,0:T(8,128)}, u32[]{:S(2)}) copy-start(f32[8,128,256]{2,1,0:T(8,128)} %refs_4_.1) | copy-start | bytes 3145732
  0.7 71.7 %copy-start.2 = (f32[8,128,256]{2,1,0:T(8,128)S(1)}, f32[8,128,256]{2,1,0:T(8,128)}, u32[]{:S(2)}) copy-start(f32[8,128,256]{2,1,0:T(8,128)} %refs_5_.1) | copy-start | bytes 3145732
  0.7 71.7 %copy-start.3 = (s32[128,1]{0,1:T(1,128)S(1)}, s32[128,1]{0,1:T(1,128)}, u32[]{:S(2)}) copy-start(s32[128,1]{0,1:T(1,128)} %param.14) | copy-start | bytes 1540
  0.7 71.7 %copy-start.4 = (s32[128,1]{0,1:T(1,128)S(1)}, s32[128,1]{0,1:T(1,128)}, u32[]{:S(2)}) copy-start(s32[128,1]{0,1:T(1,128)} %param.15) | copy-start | bytes 1540

commit v6 on v5

--- a/solution.py
+++ b/solution.py
@@ -96,10 +96,12 @@
         wide = jnp.broadcast_to(block, (self.rows, self.rows))
         return jnp.sum(jnp.where(self.eye, wide, 0.0), axis=0, keepdims=True)
 
-    def uncolumn(self, row, block):
-        wide = jnp.broadcast_to(row, (self.step, self.rows))
-        mask = self.eye[block * self.step : (block + 1) * self.step]
-        return jnp.sum(jnp.where(mask, wide, 0.0), axis=1, keepdims=True)
+    def spread(self, row):
+        return jnp.broadcast_to(row, (self.rows, self.rows)).T
+
+    def uncolumn(self, wide, block):
+        part = wide[block * self.step : (block + 1) * self.step]
+        return jnp.concatenate([part] * (self.cols // self.rows), axis=1)
 
     def fold(self, x):
         parts = [x[i * 8 : (i + 1) * 8] for i in range(self.step // 8)]
@@ -149,7 +151,7 @@
             copy.wait()
 
         def body(layer, carry):
-            south_row = self.col_in[0, 0, pl.ds(layer, 1), :]
+            south_row = self.spread(self.col_in[0, 0, pl.ds(layer, 1), :])
             for b in range(self.blocks):
                 at = pl.ds(b * step, step)
                 north = self.north[layer, at, :]
@@ -223,8 +225,8 @@
 
         def body(layer, carry):
             odd, even = carry
-            south_row = self.col_in[j + 1, 0, pl.ds(layer, 1), :]
-            north_row = self.col_in[j + 1, 1, pl.ds(layer, 1), :]
+            south_row = self.spread(self.col_in[j + 1, 0, pl.ds(layer, 1), :])
+            north_row = self.spread(self.col_in[j + 1, 1, pl.ds(layer, 1), :])
             higher = jnp.minimum(layer + 1, layers - 1)
             lower = jnp.maximum(layer - 1, 0)
             for b in range(self.blocks):
@@ -453,7 +455,7 @@
     own_weight = pltpu.make_async_copy(weight_v, weight_s.at[0, 0], move_sem.at[1])
     own_weight.start()
 
-    offsets = [(d, c) for d in range(4) for c in range(lay.cores) if (d, c) != (0, 0)]
+    offsets = [(1, 0), (3, 1), (2, 0), (2, 1), (1, 1), (3, 0), (0, 1)]
 
     def moved(axis, d, c):
         return lay.moved(**{"d" + axis: d, "dc": c})
@@ -539,7 +541,7 @@
         lax.fori_loop(0, 8, reduce, 0)
         some = pl.ds(2 * half, 2)
         mine = []
-        for d in range(1, 4):
+        for d in (1, 3, 2):
             copy = remote(summed[q].at[(me[order[1]] + d) % 4, some], landed[q].at[d - 1, some],
                           send2.at[half, q, d - 1], recv2.at[half, q, d - 1],
                           moved(order[1], d, 0))
@@ -591,7 +593,7 @@
 
         lax.fori_loop(0, 4, reduce, 0)
         mine = []
-        for d in range(1, 4):
+        for d in (1, 3, 2):
             copy = remote(second[q].at[(me[order[2]] + d) % 4], third[q].at[d - 1],
                           send3.at[q, d - 1], recv3.at[q, d - 1], moved(order[2], d, 0))
             copy.start()
@@ -601,6 +603,8 @@
         copy.wait()
     solve.apply(1, 3, solve.layers)
     early = solve.send(2, 3, solve.layers, True)
+    if common:
+        common.place(surface)
     for q, order in enumerate(ORDERS):
         for copy in copies3[q]:
             copy.wait()
@@ -608,9 +612,8 @@
             total = second[q][me[order[2]], s]
             for d in range(3):
                 total = total + third[q][d, s]
-            surface[pl.ds(*parts[q]), s * side : (s + 1) * side] = total
-    if common:
-        common.add(surface)
+            spot = (pl.ds(*parts[q]), slice(s * side, (s + 1) * side))
+            surface[spot] = surface[spot] + total if common else total
     return early
 
 
@@ -618,7 +621,7 @@
     def __init__(self, lay, me, held, weight_v, weight_in, spare, pieces, sums, others, whole,
                  send_a, recv_a, send_b, recv_b, send_c, recv_c):
         self.__dict__.update(locals())
-        self.offsets = [(d, c) for d in range(4) for c in range(2) if (d, c) != (0, 0)]
+        self.offsets = [(1, 0), (3, 1), (2, 0), (2, 1), (1, 1), (3, 0), (0, 1)]
         self.wide = lay.stages()[1]
 
     def piece(self, d, c):
@@ -673,7 +676,7 @@
         for copy in self.copies:
             copy.start()
 
-    def add(self, surface):
+    def place(self, surface):
         for copy in self.copies:
             copy.wait()
         me = self.me
@@ -683,7 +686,7 @@
         for k in range(8):
             for s in range(2):
                 at = (slice(16 * k, 16 * (k + 1)), slice(128 * s, 128 * (s + 1)))
-                surface[at] = surface[at] + mine * self.whole[k, s]
+                surface[at] = mine * self.whole[k, s]
 
 
 def exchange_scratch(cap, side):
@@ -756,7 +759,7 @@
             late = solve.send(j + 1, 0, j + 2, False)
     weight_v = exchange_refs[8]
     total = solve.total(weight_v[6:7, :])
-    sums[...] = total
+    sums[...] = jnp.where(total[6:7, 0:1] > 0.0, 1, 0)
     solve.finish(total, solution, residual, outs, leave_sem)
 
 
@@ -795,7 +798,7 @@
     return pl.pallas_call(
         functools.partial(kernel, lay, count_x, count_y, cap, (len(solve), len(moving))),
         out_shape=[jax.ShapeDtypeStruct((layers, rows, cols), jnp.float32)] * 2
-        + [jax.ShapeDtypeStruct((8, 128), jnp.float32)],
+        + [jax.ShapeDtypeStruct((1, 1), jnp.int32)],
         in_specs=[pl.BlockSpec(memory_space=pltpu.VMEM)] * 2
         + [pl.BlockSpec(memory_space=pl.ANY)] * (1 + len(grids)),
         out_specs=[pl.BlockSpec(memory_space=pl.ANY)] * 2
@@ -822,7 +825,7 @@
     def general(args, quick):
         return tuple(run(lay, count_x, count_y, 2, *args)[:2])
 
-    return move(*lax.cond(sums[6, 0] > 0.0, general, lambda args, quick: quick, args, tuple(quick)))
+    return move(*lax.cond(sums[0, 0] > 0, general, lambda args, quick: quick, args, tuple(quick)))
 
 
 def solution(mesh):

time: 75.1 us -> 74.4 us (level)
  no operation moved by 1% of the time
where the time goes in v6:
time: 74.4 us; the launch traced here: 74 us
  Pallas kernels  72.6 us (98%)
  between operations  1.35 us (2%)
    pallas_call x1, Pallas kernels, run(): pl.pallas_call(functools.partial(kernel, lay, count_x, count_y, cap, (len...  70.1 us
    pallas_call x1, Pallas kernels, move(): pl.pallas_call(move_kernel, out_shape=[jax.ShapeDtypeStruct(x.shape, x.dt...  2.57 us

profile of v6, /device:TPU:1, one launch (start us, length us, event | category | flops | bytes accessed | tf_op | source)
XLA Modules:
  0.0 74.0 jit_solution(10690918407213662485)
XLA Ops:
  0.6 0.0 copy-start
  0.6 0.0 copy-start.1
  0.7 0.0 copy-start.2
  0.7 0.0 copy-start.3
  0.7 0.0 copy-start.4
  0.7 70.1 %shard_map.113 = (f32[8,128,256]{2,1,0:T(8,128)}, f32[8,128,256]{2,1,0:T(8,128)}, s32[1,1]{1,0:T(1,128)}) custom-call(s32[1,128]{1,0:T(1,128)} %bitcast.3, s32[1,128]{1,0:T(1,128)} %bitcast.5, bf16[128,128,128]{2,1,0:T(8,128)(2,1)} %refs_2_.1, f32[8,128,256]{2,1,0:T(8,128)} %refs_3_.1, f32[8,128,256]{2,1,0:T(8,128)} %refs_4_.1, f32[8,128,256]{2,1,0:T(8,128)} %refs_5_.1, ...), custom_call_target="tpu_custom_call" | custom-call | tf_op jit(solution)/shard_map/pallas_call | solution.py:798
  71.4 0.0 copy-done
  71.4 0.0 copy-done.1
  71.4 0.0 copy-done.2
  71.4 0.0 copy-done.3
  71.4 0.0 copy-done.4
  71.4 2.6 %shard_map.114 = (f32[8,128,256]{2,1,0:T(8,128)}, f32[8,128,256]{2,1,0:T(8,128)}) custom-call(f32[8,128,256]{2,1,0:T(8,128)} %get-tuple-element.46.a, f32[8,128,256]{2,1,0:T(8,128)} %get-tuple-element.47.b), custom_call_target="tpu_custom_call" | custom-call | tf_op jit(solution)/shard_map/pallas_call | solution.py:783
  (1 shorter events, 0.0 us)
Async XLA Ops:
  0.6 70.7 %copy-start = (f32[8,128,256]{2,1,0:T(8,128)S(1)}, f32[8,128,256]{2,1,0:T(8,128)}, u32[]{:S(2)}) copy-start(f32[8,128,256]{2,1,0:T(8,128)} %refs_3_.1) | copy-start | bytes 3145732
  0.6 70.7 %copy-start.1 = (f32[8,128,256]{2,1,0:T(8,128)S(1)}, f32[8,128,256]{2,1,0:T(8,128)}, u32[]{:S(2)}) copy-start(f32[8,128,256]{2,1,0:T(8,128)} %refs_4_.1) | copy-start | bytes 3145732
  0.7 70.7 %copy-start.2 = (f32[8,128,256]{2,1,0:T(8,128)S(1)}, f32[8,128,256]{2,1,0:T(8,128)}, u32[]{:S(2)}) copy-start(f32[8,128,256]{2,1,0:T(8,128)} %refs_5_.1) | copy-start | bytes 3145732
  0.7 70.7 %copy-start.3 = (s32[128,1]{0,1:T(1,128)S(1)}, s32[128,1]{0,1:T(1,128)}, u32[]{:S(2)}) copy-start(s32[128,1]{0,1:T(1,128)} %param.14) | copy-start | bytes 1540
  0.7 70.7 %copy-start.4 = (s32[128,1]{0,1:T(1,128)S(1)}, s32[128,1]{0,1:T(1,128)}, u32[]{:S(2)}) copy-start(s32[128,1]{0,1:T(1,128)} %param.15) | copy-start | bytes 1540

commit v7 on v6

--- a/solution.py
+++ b/solution.py
@@ -268,7 +268,7 @@
             partial[0, k : k + 1, :] = jnp.sum(both, axis=0, keepdims=True)
         partial[0, 6:7, :] = extra
         base = 0
-        for s, peers in enumerate(self.lay.stages()):
+        for s, peers in enumerate(reversed(self.lay.stages())):
             copies = [
                 remote(partial.at[s], gathered.at[base + i], self.sum_send.at[base + i],
                        self.sum_recv.at[base + i], self.lay.moved(**offset))

time: 74.4 us -> 74.2 us (level)
  no operation moved by 1% of the time
where the time goes in v7:
time: 74.2 us; the launch traced here: 74.1 us
  Pallas kernels  72.7 us (98%)
  between operations  1.35 us (2%)
    pallas_call x1, Pallas kernels, run(): pl.pallas_call(functools.partial(kernel, lay, count_x, count_y, cap, (len...  70.1 us
    pallas_call x1, Pallas kernels, move(): pl.pallas_call(move_kernel, out_shape=[jax.ShapeDtypeStruct(x.shape, x.dt...  2.57 us

profile of v7, /device:TPU:1, one launch (start us, length us, event | category | flops | bytes accessed | tf_op | source)
XLA Modules:
  0.0 74.1 jit_solution(779764127759143259)
XLA Ops:
  0.6 0.0 copy-start
  0.6 0.0 copy-start.1
  0.7 0.0 copy-start.2
  0.7 0.0 copy-start.3
  0.7 0.0 copy-start.4
  0.7 70.1 %shard_map.113 = (f32[8,128,256]{2,1,0:T(8,128)}, f32[8,128,256]{2,1,0:T(8,128)}, s32[1,1]{1,0:T(1,128)}) custom-call(s32[1,128]{1,0:T(1,128)} %bitcast.3, s32[1,128]{1,0:T(1,128)} %bitcast.5, bf16[128,128,128]{2,1,0:T(8,128)(2,1)} %refs_2_.1, f32[8,128,256]{2,1,0:T(8,128)} %refs_3_.1, f32[8,128,256]{2,1,0:T(8,128)} %refs_4_.1, f32[8,128,256]{2,1,0:T(8,128)} %refs_5_.1, ...), custom_call_target="tpu_custom_call" | custom-call | tf_op jit(solution)/shard_map/pallas_call | solution.py:798
  71.5 0.0 copy-done
  71.5 0.0 copy-done.1
  71.5 0.0 copy-done.2
  71.5 0.0 copy-done.3
  71.5 0.0 copy-done.4
  71.5 2.6 %shard_map.114 = (f32[8,128,256]{2,1,0:T(8,128)}, f32[8,128,256]{2,1,0:T(8,128)}) custom-call(f32[8,128,256]{2,1,0:T(8,128)} %get-tuple-element.46.a, f32[8,128,256]{2,1,0:T(8,128)} %get-tuple-element.47.b), custom_call_target="tpu_custom_call" | custom-call | tf_op jit(solution)/shard_map/pallas_call | solution.py:783
  (1 shorter events, 0.0 us)
Async XLA Ops:
  0.6 70.8 %copy-start = (f32[8,128,256]{2,1,0:T(8,128)S(1)}, f32[8,128,256]{2,1,0:T(8,128)}, u32[]{:S(2)}) copy-start(f32[8,128,256]{2,1,0:T(8,128)} %refs_3_.1) | copy-start | bytes 3145732
  0.6 70.8 %copy-start.1 = (f32[8,128,256]{2,1,0:T(8,128)S(1)}, f32[8,128,256]{2,1,0:T(8,128)}, u32[]{:S(2)}) copy-start(f32[8,128,256]{2,1,0:T(8,128)} %refs_4_.1) | copy-start | bytes 3145732
  0.7 70.8 %copy-start.2 = (f32[8,128,256]{2,1,0:T(8,128)S(1)}, f32[8,128,256]{2,1,0:T(8,128)}, u32[]{:S(2)}) copy-start(f32[8,128,256]{2,1,0:T(8,128)} %refs_5_.1) | copy-start | bytes 3145732
  0.7 70.8 %copy-start.3 = (s32[128,1]{0,1:T(1,128)S(1)}, s32[128,1]{0,1:T(1,128)}, u32[]{:S(2)}) copy-start(s32[128,1]{0,1:T(1,128)} %param.14) | copy-start | bytes 1540
  0.7 70.8 %copy-start.4 = (s32[128,1]{0,1:T(1,128)S(1)}, s32[128,1]{0,1:T(1,128)}, u32[]{:S(2)}) copy-start(s32[128,1]{0,1:T(1,128)} %param.15) | copy-start | bytes 1540
